TPU v7x, 256 devices: a whole 4x4x8 slice. The times are simulated.
256 devices in a mesh: dp: 4 (over y), expert: 64 (over z, x, core).
Axes of the slice: x: 4, y: 4, z: 8, core: 2. Of those that a mesh axis runs over, the one named last changes fastest.
Arguments:
- tokens: bfloat16 [32768, 3584], P(('dp', 'expert')), may hold values from -24 to 24
- cotangent: bfloat16 [32768, 3584], P(('dp', 'expert')), may hold values from -0.375 to 0.375
- gate_scale: float32 [32768], P(('dp', 'expert')), may hold values from 0.2 to 1
- expert_index: int32 [32768], P(('dp', 'expert')), may hold values from 0 to 63, as said below
- hot_index: int32 [64], replicated, may hold values from 0 to 63, as said below
- w_gate: bfloat16 [64, 3584, 1024], P('expert', None, 'dp'), may hold values from -0.09375 to 0.09375
- w_up: bfloat16 [64, 3584, 1024], P('expert', None, 'dp'), may hold values from -0.09375 to 0.09375
- w_down: bfloat16 [64, 1024, 3584], P('expert', 'dp'), may hold values from -0.1875 to 0.1875
Outputs:
- grad_gate: bfloat16 [64, 3584, 1024], P('expert', None, 'dp')
- grad_up: bfloat16 [64, 3584, 1024], P('expert', None, 'dp')
- grad_down: bfloat16 [64, 1024, 3584], P('expert', 'dp')
- hot_grads: bfloat16 [1, 3584, 3, 1024], P(None, 'expert', None, 'dp')
Inputs may be any that keep to these rules, and one draw needn't show every extreme that they name: `expert_index`: among the 128 tokens of one device (aligned blocks of rows), at most 3 are routed to any one expert other than hot_index[0], and from 3 to 6 to hot_index[0]. In every draw each group of devices sharing a dp index has an expert that receives exactly 3 tokens from each of its devices, and some devices route exactly 6 tokens to hot_index[0]. `hot_index`: A permutation of the 64 experts; its first entry is the replicated expert, to which every device routes at least as many tokens as to any other expert.
All inputs are finite; a program needn't handle non-finite values.
Results may differ from a plain program's by a relative error of at most 0.0058.
Values may be sent and summed in bfloat16 or wider, within the bound.
A program may use at most 128 MiB of HBM per device.

v0:
```python
import jax
import jax.numpy as jnp
from jax import lax
from jax.sharding import PartitionSpec as P

CONTRACT_ROWS = (((0,), (0,)), ((), ()))


def spread(block, axis, source):
    block = jnp.where(lax.axis_index(axis) == source, block, jnp.zeros_like(block))
    return lax.psum(block, axis)


def expert_terms(row_tokens, row_grads, gate_matrix, up_matrix, down_matrix):
    pre_gate = jnp.dot(row_tokens, gate_matrix, preferred_element_type=jnp.float32)
    pre_up = jnp.dot(row_tokens, up_matrix, preferred_element_type=jnp.float32)
    hidden_back = lax.dot_general(
        row_grads, down_matrix, (((1,), (1,)), ((), ())), preferred_element_type=jnp.float32
    )
    sigmoid_gate = jax.nn.sigmoid(pre_gate)
    activated = pre_gate * sigmoid_gate
    hidden = (activated * pre_up).astype(jnp.bfloat16)
    gate_grad = (
        hidden_back * pre_up * sigmoid_gate * (1.0 + pre_gate * (1.0 - sigmoid_gate))
    ).astype(jnp.bfloat16)
    up_grad = (hidden_back * activated).astype(jnp.bfloat16)
    return (hidden, gate_grad, up_grad)


def column_sum(left, right):
    return lax.dot_general(left, right, CONTRACT_ROWS, preferred_element_type=jnp.float32)


def route_rows(selector, values):
    return jnp.dot(selector, values, preferred_element_type=jnp.float32).astype(jnp.bfloat16)


def on_device(tokens, cotangent, gate_scale, expert_index, hot_index, w_gate, w_up, w_down):
    tok_rows, feature_width = tokens.shape
    experts = lax.axis_size("expert")
    capacity = 3 * tok_rows // (2 * experts)
    hot_capacity = 2 * capacity
    hot_expert = hot_index[0]
    route_grad = (gate_scale[:, None] * cotangent.astype(jnp.float32)).astype(jnp.bfloat16)
    is_hot = expert_index == hot_expert
    not_hot = jnp.logical_not(is_hot)
    owners = lax.broadcasted_iota(jnp.int32, (tok_rows, experts), 1)
    member = ((expert_index[:, None] == owners) & not_hot[:, None]).astype(jnp.int32)
    bucket_place = jnp.sum((jnp.cumsum(member, axis=0) - 1) * member, axis=1)
    slot_index = expert_index * capacity + bucket_place
    slot_grid = lax.broadcasted_iota(jnp.int32, (experts * capacity, tok_rows), 0)
    cold_map = ((slot_grid == slot_index[None, :]) & not_hot[None, :]).astype(jnp.bfloat16)
    hot_place = jnp.cumsum(is_hot.astype(jnp.int32)) - 1
    hot_grid = lax.broadcasted_iota(jnp.int32, (hot_capacity, tok_rows), 0)
    hot_map = ((hot_grid == hot_place[None, :]) & is_hot[None, :]).astype(jnp.bfloat16)
    send_tokens = route_rows(cold_map, tokens).reshape(experts, capacity, feature_width)
    send_grads = route_rows(cold_map, route_grad).reshape(experts, capacity, feature_width)
    own_hot_tokens = route_rows(hot_map, tokens)
    own_hot_grads = route_rows(hot_map, route_grad)
    arrived_tokens, arrived_grads = (
        lax.all_to_all(send_tokens, "expert", split_axis=0, concat_axis=0, tiled=True),
        lax.all_to_all(send_grads, "expert", split_axis=0, concat_axis=0, tiled=True),
    )
    cold_tokens, cold_grads, hot_tokens, hot_row_grads = (
        lax.all_gather(
            arrived_tokens.reshape(experts * capacity, feature_width), "dp", axis=0, tiled=True
        ),
        lax.all_gather(
            arrived_grads.reshape(experts * capacity, feature_width), "dp", axis=0, tiled=True
        ),
        lax.all_gather(own_hot_tokens, "dp", axis=0, tiled=True),
        lax.all_gather(own_hot_grads, "dp", axis=0, tiled=True),
    )
    shadow_gate, shadow_up, shadow_down = (
        spread(w_gate[0], "expert", hot_expert),
        spread(w_up[0], "expert", hot_expert),
        spread(w_down[0], "expert", hot_expert),
    )
    hidden, gate_grad, up_grad = expert_terms(
        cold_tokens, cold_grads, w_gate[0], w_up[0], w_down[0]
    )
    grad_gate = column_sum(cold_tokens, gate_grad).astype(jnp.bfloat16)
    grad_up = column_sum(cold_tokens, up_grad).astype(jnp.bfloat16)
    grad_down = column_sum(hidden, cold_grads).astype(jnp.bfloat16)
    hot_hidden, hot_gate_grad, hot_up_grad = expert_terms(
        hot_tokens, hot_row_grads, shadow_gate, shadow_up, shadow_down
    )
    gate_part = column_sum(hot_tokens, hot_gate_grad)
    up_part = column_sum(hot_tokens, hot_up_grad)
    down_part = column_sum(hot_row_grads, hot_hidden)
    owned_part = lax.psum_scatter(
        jnp.stack([gate_part, up_part, down_part], axis=1),
        "expert",
        scatter_dimension=0,
        tiled=True,
    )
    hot_grads = owned_part.astype(jnp.bfloat16)[None]
    return (grad_gate[None], grad_up[None], grad_down[None], hot_grads)


def solution(mesh):
    placed = (
        P(("dp", "expert"), None),
        P(("dp", "expert"), None),
        P(("dp", "expert")),
        P(("dp", "expert")),
        P(),
        P("expert", None, "dp"),
        P("expert", None, "dp"),
        P("expert", "dp", None),
    )
    return jax.shard_map(
        on_device,
        mesh=mesh,
        in_specs=placed,
        out_specs=(
            P("expert", None, "dp"),
            P("expert", None, "dp"),
            P("expert", "dp", None),
            P(None, "expert", None, "dp"),
        ),
        check_vma=False,
    )
```

profile of v0, /device:TPU:1, one launch (start us, length us, event | category | flops | bytes accessed | tf_op | source)
XLA Modules:
  0.0 425.0 jit_solution(13762567251531066128)
XLA Ops:
  8.8 3.0 bitcast_select_fusion.2
  11.8 2.1 bitcast_select_fusion
  14.0 0.6 copy-done.11
  15.1 1.6 convolution_convert_fusion.4
  16.7 2.6 reshape.54
  19.3 66.8 %all_to_all.10 = bf16[64,3,3584]{2,1,0:T(4,128)(2,1)} all-to-all(bf16[64,3,3584]{2,1,0:T(4,128)(2,1)S(1)} %reshape.54), channel_id=1, replica_groups=mesh['dp'=4,'expert'=64] {'expert'}, dimensions={0} | all-to-all | bytes 2752512 | tf_op jit(solution)/shard_map/all_to_all | solution.py:61
  86.1 4.2 reshape.55
  90.4 1.7 convolution_convert_fusion.3
  92.1 2.6 reshape.56
  94.7 53.4 %all_to_all.11 = bf16[64,3,3584]{2,1,0:T(4,128)(2,1)} all-to-all(bf16[64,3,3584]{2,1,0:T(4,128)(2,1)S(1)} %reshape.56), channel_id=1, replica_groups=mesh['dp'=4,'expert'=64] {'expert'}, dimensions={0} | all-to-all | bytes 2752512 | tf_op jit(solution)/shard_map/all_to_all | solution.py:62
  148.1 4.1 reshape.57
  152.9 9.6 %all-gather = bf16[4,6,3584]{2,1,0:T(8,128)(2,1)S(1)} all-gather(bf16[1,6,3584]{2,1,0:T(8,128)(2,1)S(1)} %fusion.3), channel_id=1, replica_groups=mesh['dp'=4,'expert'=64] {'dp'}, dimensions={0}, use_global_device_ids=true | all-gather | bytes 215040 | tf_op jit(solution)/shard_map/all_gather | solution.py:71
  162.9 11.0 %all-gather.1 = bf16[4,6,3584]{2,1,0:T(8,128)(2,1)S(1)} all-gather(bf16[1,6,3584]{2,1,0:T(8,128)(2,1)S(1)} %fusion.4), channel_id=1, replica_groups=mesh['dp'=4,'expert'=64] {'dp'}, dimensions={0}, use_global_device_ids=true | all-gather | bytes 215040 | tf_op jit(solution)/shard_map/all_gather | solution.py:72
  174.0 76.6 %all-reduce.3.cloned.1.call-done = (bf16[3584,256]{1,0:T(8,128)(2,1)}, bf16[3584,256]{1,0:T(8,128)(2,1)}, bf16[256,3584]{1,0:T(8,128)(2,1)}) async-done(((bf16[3584,256]{1,0:T(8,128)(2,1)}, bf16[3584,256]{1,0:T(8,128)(2,1)}, bf16[256,3584]{1,0:T(8,128)(2,1)}), (bf16[3584,256]{1,0:T(8,128)(2,1)}, bf16[3584,256]{1,0:T(8,128)(2,1)}, bf16[256,3584]{1,0:T(8,128)(2,1)})) %all-reduce.3.cloned.1.call-update) | async-done | bytes 5505040 | tf_op jit(solution)/shard_map/psum | solution.py:11
  250.6 2.0 fusion.43
  252.7 0.4 fusion.42
  253.0 0.7 convolution_bitcast_fusion
  253.7 0.8 copy-done.5
  254.5 0.6 fusion.41
  255.1 0.7 convolution_bitcast_fusion.1
  255.8 0.7 convolution_bitcast_fusion.2
  256.5 4.9 %pad_maximum_fusion = f32[3584,3,256]{2,0,1:T(8,128)} fusion(f32[3584,1,256]{2,0,1:T(8,128)S(1)} %convolution_bitcast_fusion, f32[3584,1,256]{2,0,1:T(8,128)S(1)} %convolution_bitcast_fusion.1, f32[3584,1,256]{2,0,1:T(8,128)S(1)} %convolution_bitcast_fusion.2), kind=kLoop, calls=%fused_computation | loop fusion | flops 5505024 | bytes 22020096 | tf_op jit(solution)/shard_map/stack | solution.py:92
  261.5 1.4 copy-done.8
  262.9 4.3 %fusion.5 = f32[768,256]{1,0:T(8,128)S(1)} fusion(bf16[768,3584]{1,0:T(8,128)(2,1)} %all-gather.5.cloned.1.call-done, bf16[1,3584,256]{2,1,0:T(8,128)(2,1)S(1)} %copy-done.8), kind=kOutput, calls=%fused_computation.17 | convolution fusion | flops 1409286144 | bytes 8126464 | tf_op jit(solution)/shard_map/dot_general | solution.py:15
  267.2 0.4 copy-done.14
  267.6 1.6 fusion.7
  269.3 4.4 %fusion.9 = f32[768,256]{1,0:T(8,128)S(1)} fusion(bf16[768,3584]{1,0:T(8,128)(2,1)} %all-gather.7.cloned.1.call-done, bf16[1,256,3584]{2,1,0:T(8,128)(2,1)S(1)} %copy-done.4), kind=kOutput, calls=%fused_computation.23 | convolution fusion | flops 1409286144 | bytes 8126464 | tf_op jit(solution)/shard_map/dot_general | solution.py:17
  273.8 3.0 fusion.2
  276.8 3.1 fusion.1
  279.9 3.2 fusion
  283.1 132.9 %reduce-scatter.2.cloned.1.call-done = f32[56,3,256]{2,0,1:T(8,128)} async-done(((f32[3584,3,256]{2,0,1:T(8,128)}), f32[56,3,256]{2,0,1:T(8,128)}) %reduce-scatter.2.cloned.1.call-update) | async-done | bytes 172048 | tf_op jit(solution)/shard_map/reduce_scatter | solution.py:91
  416.0 1.6 convert_bitcast_fusion
  (60 shorter events, 2.1 us)
Async XLA Ops:
  8.0 7.1 %copy-start = (bf16[128,3584]{1,0:T(8,128)(2,1)S(1)}, bf16[128,3584]{1,0:T(8,128)(2,1)}, u32[]{:S(2)}) copy-start(bf16[128,3584]{1,0:T(8,128)(2,1)} %param.8) | copy-start | bytes 2752516
  8.0 242.6 %all-reduce.3.cloned.1.call-start = ((), (), s32[]{:S(2)}) async-start(), calls=%async_computation.6 | async-start | bytes 11010048 | tf_op jit(solution)/shard_map/psum | solution.py:11
  8.8 3.0 copy-start.7
  8.8 3.0 copy-start.9
  13.9 0.7 copy-start.11
  13.9 0.7 copy-start.13
  13.9 247.5 %all-gather.5.cloned.1.call-start = ((), (), s32[]{:S(2)}) async-start(), calls=%async_computation.3 | async-start | bytes 6881280 | tf_op jit(solution)/shard_map/all_gather | solution.py:65
  86.1 4.3 %copy-start.2 = (bf16[128,3584]{1,0:T(8,128)(2,1)S(1)}, bf16[128,3584]{1,0:T(8,128)(2,1)}, u32[]{:S(2)}) copy-start(bf16[128,3584]{1,0:T(8,128)(2,1)} %param.9) | copy-start | bytes 2752516
  86.1 4.3 %copy-start.12 = (f32[128]{0:T(128)S(1)}, f32[128]{0:T(128)}, u32[]{:S(2)}) copy-start(f32[128]{0:T(128)} %param.10) | copy-start | bytes 1540
  90.3 178.9 %all-gather.7.cloned.1.call-start = ((), (), s32[]{:S(2)}) async-start(), calls=%async_computation.4 | async-start | bytes 6881280 | tf_op jit(solution)/shard_map/all_gather | solution.py:68
  152.2 10.4 %copy-start.3 = (bf16[128,3584]{1,0:T(8,128)(2,1)S(1)}, bf16[128,3584]{1,0:T(8,128)(2,1)}, u32[]{:S(2)}) copy-start(bf16[128,3584]{1,0:T(8,128)(2,1)} %param.9) | copy-start | bytes 2752516
  152.2 263.8 %reduce-scatter.2.cloned.1.call-start = ((), (), s32[]{:S(2)}) async-start(), calls=%async_computation.5 | async-start | bytes 11182080 | tf_op jit(solution)/shard_map/reduce_scatter | solution.py:91
  250.6 2.1 copy-start.6
  253.0 1.5 copy-start.5
  261.4 1.5 copy-start.8
  262.9 4.3 %copy-start.10 = (bf16[1,3584,256]{2,1,0:T(8,128)(2,1)S(1)}, bf16[1,3584,256]{2,1,0:T(8,128)(2,1)}, u32[]{:S(2)}) copy-start(bf16[1,3584,256]{2,1,0:T(8,128)(2,1)} %param.14) | copy-start | bytes 5505028
  262.9 4.7 %copy-start.14 = (bf16[768,3584]{1,0:T(8,128)(2,1)S(1)}, bf16[768,3584]{1,0:T(8,128)(2,1)}, u32[]{:S(2)}) copy-start(bf16[768,3584]{1,0:T(8,128)(2,1)} %all-gather.5.cloned.1.call-done) | copy-start | bytes 16515076
  267.6 1.6 copy-start.4
  269.2 4.5 %copy-start.16 = (f32[768,256]{1,0:T(8,128)}, f32[768,256]{1,0:T(8,128)S(1)}, u32[]{:S(2)}) copy-start(f32[768,256]{1,0:T(8,128)S(1)} %fusion.7) | copy-start | bytes 2359300
  269.3 4.6 %copy-start.15 = (bf16[768,3584]{1,0:T(8,128)(2,1)S(1)}, bf16[768,3584]{1,0:T(8,128)(2,1)}, u32[]{:S(2)}) copy-start(bf16[768,3584]{1,0:T(8,128)(2,1)} %all-gather.7.cloned.1.call-done) | copy-start | bytes 16515076
  269.3 7.5 %slice-start = ((s8[5505024]{0:T(1024)(128)(4,1)}), s8[4194304]{0:T(1024)(128)(4,1)S(1)}, s32[]{:S(2)}) async-start(s8[5505024]{0:T(1024)(128)(4,1)} %bitcast.53), calls=%async_computation.7 | async-start | bytes 8388608
  273.8 3.0 slice-start.1
  276.8 3.1 copy-start.17
  279.9 137.6 %copy-start.1 = (bf16[128,3584]{1,0:T(8,128)(2,1)S(1)}, bf16[128,3584]{1,0:T(8,128)(2,1)}, u32[]{:S(2)}) copy-start(bf16[128,3584]{1,0:T(8,128)(2,1)} %param.8) | copy-start | bytes 2752516
Sparse Core Ops, SparseCore 0:
  14.0 236.5 all-reduce.2
  261.5 154.4 reduce-scatter.1
Sparse Core Ops, SparseCore 1:
  90.4 59.1 all-gather.4
  152.3 62.5 all-gather.6
where the time goes:
time: 429 us; the launch traced here: 425 us
  waiting for transfers between devices  210 us (49%)
  blocking collectives  141 us (33%)
  matrix products  28.5 us (7%)
  local copies, waits for them, and re-layouts  17.2 us (4%)
  between operations  16.5 us (4%)
  other arithmetic  12.3 us (3%)
    reduce_scatter x1, waiting for transfers between devices, on_device(): lax.psum_scatter(jnp.stack([gate_part, up_part, down_part], axis=1), 'exp...  133 us
    psum x1, waiting for transfers between devices, spread(): return lax.psum(block, axis)  76.6 us
    all_to_all x1, blocking collectives, on_device(): lax.all_to_all(send_tokens, 'expert', split_axis=0, concat_axis=0, tiled=...  66.8 us
    all_to_all x1, blocking collectives, on_device(): lax.all_to_all(send_grads, 'expert', split_axis=0, concat_axis=0, tiled=T...  53.4 us
    dot_general x6, matrix products, column_sum(): lax.dot_general(left, right, CONTRACT_ROWS, preferred_element_type=jnp.fl...  11.4 us
    all_gather x1, blocking collectives, on_device(): lax.all_gather(own_hot_grads, 'dp', axis=0, tiled=True)  11 us
    all_gather x1, blocking collectives, on_device(): lax.all_gather(own_hot_tokens, 'dp', axis=0, tiled=True)  9.61 us
  transfers between devices with their start and end apart: 4, of which 2 were waited for; matrix products, arithmetic and copies ran while one was open for 11% of the time, Pallas kernels for 0%

commit v1 on v0

v1 whole, which is shorter than its diff:
```python
import jax
import jax.numpy as jnp
from jax import lax
from jax.experimental import pallas as pl
from jax.experimental.pallas import tpu as pltpu
from jax.sharding import PartitionSpec as P

CONTRACT_ROWS = (((0,), (0,)), ((), ()))
MESH = pl.DeviceIdType.MESH
PIECES = 8


def spread(block, axis, source):
    block = jnp.where(lax.axis_index(axis) == source, block, jnp.zeros_like(block))
    return lax.psum(block, axis)


def expert_terms(row_tokens, row_grads, gate_matrix, up_matrix, down_matrix):
    pre_gate = jnp.dot(row_tokens, gate_matrix, preferred_element_type=jnp.float32)
    pre_up = jnp.dot(row_tokens, up_matrix, preferred_element_type=jnp.float32)
    hidden_back = lax.dot_general(
        row_grads, down_matrix, (((1,), (1,)), ((), ())), preferred_element_type=jnp.float32
    )
    sigmoid_gate = jax.nn.sigmoid(pre_gate)
    activated = pre_gate * sigmoid_gate
    hidden = (activated * pre_up).astype(jnp.bfloat16)
    gate_grad = (
        hidden_back * pre_up * sigmoid_gate * (1.0 + pre_gate * (1.0 - sigmoid_gate))
    ).astype(jnp.bfloat16)
    up_grad = (hidden_back * activated).astype(jnp.bfloat16)
    return (hidden, gate_grad, up_grad)


def column_sum(left, right):
    return lax.dot_general(left, right, CONTRACT_ROWS, preferred_element_type=jnp.float32)


def route_rows(selector, values):
    return jnp.dot(selector, values, preferred_element_type=jnp.float32).astype(jnp.bfloat16)


def exchange_kernel(nz, nq, send, send_hot, own_hot, got, got_hot, all_hot,
                    mid, mid_hot, z_send, z_recv, q_send, q_recv, local_sem,
                    y_send, y_recv, f_send, f_recv, h_send, h_recv):
    ny = 4
    chunks = send.shape[0]
    y = lax.axis_index("dp")
    e = lax.axis_index("expert")
    z = lax.div(e, nq)
    q = lax.rem(e, nq)
    up = lax.rem(y + 1, ny)
    down = lax.rem(y + ny - 1, ny)

    def z_peer(k):
        return lax.rem(z + k, nz)

    def q_peer(k):
        return lax.rem(q + k, nq)

    def q_source(k):
        return lax.rem(q + nq - k, nq)

    barrier = pltpu.get_barrier_semaphore()
    for k in range(1, nz):
        pl.semaphore_signal(barrier, inc=1, device_id=(y, z_peer(k) * nq + q), device_id_type=MESH)
    for k in range(1, nq):
        pl.semaphore_signal(barrier, inc=1, device_id=(y, z * nq + q_peer(k)), device_id_type=MESH)
    for k in range(1, ny):
        pl.semaphore_signal(barrier, inc=1, device_id=(lax.rem(y + k, ny), e), device_id_type=MESH)
    pl.semaphore_wait(barrier, nz - 1 + nq - 1 + ny - 1)

    def z_refs(s):
        if s < chunks:
            return send.at[s], mid.at[s]
        return send_hot, mid_hot

    def q_dst(s, who):
        if s < chunks:
            return got.at[s, y, who]
        return got_hot.at[:, who, y]

    def y_block(s, who, plane):
        if s < chunks:
            return got.at[s, plane, who]
        return got_hot.at[:, who, plane]

    def z_copy(s, k):
        src, dst = z_refs(s)
        return pltpu.make_async_remote_copy(
            src_ref=src.at[z_peer(k)], dst_ref=dst.at[z],
            send_sem=z_send.at[s, k - 1], recv_sem=z_recv.at[s, k - 1],
            device_id=(y, z_peer(k) * nq + q), device_id_type=MESH)

    def z_own(s):
        src, dst = z_refs(s)
        return pltpu.make_async_copy(src.at[z], dst.at[z], local_sem.at[s, 0])

    def q_copy(s, k):
        _, src = z_refs(s)
        return pltpu.make_async_remote_copy(
            src_ref=src.at[:, q_peer(k)], dst_ref=q_dst(s, q),
            send_sem=q_send.at[s, k - 1], recv_sem=q_recv.at[s, k - 1],
            device_id=(y, z * nq + q_peer(k)), device_id_type=MESH)

    def q_own(s):
        _, src = z_refs(s)
        return pltpu.make_async_copy(src.at[:, q], q_dst(s, q), local_sem.at[s, 1])

    def y_copy(s, k, way):
        block = y_block(s, q_source(k), y)
        return pltpu.make_async_remote_copy(
            src_ref=block, dst_ref=block,
            send_sem=y_send.at[s, k, way], recv_sem=y_recv.at[s, k, way],
            device_id=(up if way == 0 else down, e), device_id_type=MESH)

    def f_copy(s, k):
        way = 0 if k < nq // 2 else 1
        block = y_block(s, q_source(k), down if way == 0 else up)
        return pltpu.make_async_remote_copy(
            src_ref=block, dst_ref=block,
            send_sem=f_send.at[s, k], recv_sem=f_recv.at[s, k],
            device_id=(up if way == 0 else down, e), device_id_type=MESH)

    def h_copy(k):
        return pltpu.make_async_remote_copy(
            src_ref=own_hot, dst_ref=all_hot.at[y],
            send_sem=h_send.at[k - 1], recv_sem=h_recv.at[k - 1],
            device_id=(lax.rem(y + k, ny), e), device_id_type=MESH)

    hot_own = pltpu.make_async_copy(own_hot, all_hot.at[y], local_sem.at[0, 2])
    hot_own.start()
    for k in range(1, ny):
        h_copy(k).start()
    z_order = sorted(range(1, nz), key=lambda k: -min(k, nz - k))
    for s in range(chunks + 1):
        z_own(s).start()
        for k in z_order:
            z_copy(s, k).start()

    def pass_on(s, k):
        way = 0 if k < nq // 2 else 1
        y_copy(s, k, way).wait_recv()
        f_copy(s, k).start()

    for s in range(chunks + 1):
        z_own(s).wait()
        for k in z_order:
            z_copy(s, k).wait_recv()
        q_own(s).start()
        for k in range(1, nq):
            q_copy(s, k).start()
        for k in range(nq):
            if k == 0:
                q_own(s).wait()
            else:
                q_copy(s, k).wait_recv()
            y_copy(s, k, 0).start()
            y_copy(s, k, 1).start()
            if s > 0:
                pass_on(s - 1, k)
    for k in range(nq):
        pass_on(chunks, k)

    hot_own.wait()
    for k in range(1, ny):
        h_copy(k).wait()
    for s in range(chunks + 1):
        for k in range(1, nz):
            z_copy(s, k).wait_send()
        for k in range(1, nq):
            q_copy(s, k).wait_send()
        for k in range(nq):
            y_copy(s, k, 0).wait_send()
            y_copy(s, k, 1).wait_send()
            y_copy(s, k, 1 if k < nq // 2 else 0).wait_recv()
            f_copy(s, k).wait()


def exchange(send, send_hot, own_hot, nz, nq):
    slots, _, _, pieces, width = send.shape
    hot_slots, hot_width = send_hot.shape[-2:]
    bf16 = jnp.bfloat16
    steps = slots + 1
    dma = pltpu.SemaphoreType.DMA

    def body(*refs):
        exchange_kernel(nz, nq, *refs)

    hbm = pl.BlockSpec(memory_space=pl.ANY)
    vmem = pl.BlockSpec(memory_space=pltpu.VMEM)
    return pl.pallas_call(
        body,
        out_shape=(
            jax.ShapeDtypeStruct((slots, 4, nq, nz, pieces, width), bf16),
            jax.ShapeDtypeStruct((nz, nq, 4, hot_slots, hot_width), bf16),
            jax.ShapeDtypeStruct((4,) + own_hot.shape, bf16),
        ),
        in_specs=[hbm, hbm, vmem],
        out_specs=(hbm, hbm, hbm),
        scratch_shapes=[
            pltpu.VMEM((slots, nz, nq, pieces, width), bf16),
            pltpu.VMEM((nz, nq, hot_slots, hot_width), bf16),
            dma((steps, nz - 1)),
            dma((steps, nz - 1)),
            dma((steps, nq - 1)),
            dma((steps, nq - 1)),
            dma((steps, 3)),
            dma((steps, nq, 2)),
            dma((steps, nq, 2)),
            dma((steps, nq)),
            dma((steps, nq)),
            dma((3,)),
            dma((3,)),
        ],
        compiler_params=pltpu.CompilerParams(
            collective_id=0, has_side_effects=True, vmem_limit_bytes=24 * 1024 * 1024
        ),
        cost_estimate=pl.CostEstimate(flops=0, bytes_accessed=300_000_000, transcendentals=0),
    )(send, send_hot, own_hot)


def on_device(tokens, cotangent, gate_scale, expert_index, hot_index, w_gate, w_up, w_down):
    tok_rows, feature_width = tokens.shape
    experts = lax.axis_size("expert")
    nq = 8 if experts == 64 else 2
    nz = experts // nq
    capacity = 3 * tok_rows // (2 * experts)
    hot_slots = 8
    hot_expert = hot_index[0]
    route_grad = (gate_scale[:, None] * cotangent.astype(jnp.float32)).astype(jnp.bfloat16)
    both = jnp.concatenate([tokens, route_grad], axis=1)
    is_hot = expert_index == hot_expert
    not_hot = jnp.logical_not(is_hot)
    owners = lax.broadcasted_iota(jnp.int32, (tok_rows, experts), 1)
    member = ((expert_index[:, None] == owners) & not_hot[:, None]).astype(jnp.int32)
    bucket_place = jnp.sum((jnp.cumsum(member, axis=0) - 1) * member, axis=1)
    slot_index = bucket_place * experts + expert_index
    slot_grid = lax.broadcasted_iota(jnp.int32, (experts * capacity, tok_rows), 0)
    cold_map = ((slot_grid == slot_index[None, :]) & not_hot[None, :]).astype(jnp.bfloat16)
    hot_place = jnp.cumsum(is_hot.astype(jnp.int32)) - 1
    hot_grid = lax.broadcasted_iota(jnp.int32, (hot_slots, tok_rows), 0)
    hot_map = ((hot_grid == hot_place[None, :]) & is_hot[None, :]).astype(jnp.bfloat16)
    send = route_rows(cold_map, both)
    own_hot = route_rows(hot_map, both)
    part = feature_width // experts
    hot_width = -(-2 * part // 128) * 128
    send_hot = jnp.concatenate(
        [
            own_hot[:, :feature_width].reshape(hot_slots, experts, part),
            own_hot[:, feature_width:].reshape(hot_slots, experts, part),
            jnp.zeros((hot_slots, experts, hot_width - 2 * part), jnp.bfloat16),
        ],
        axis=2,
    ).transpose(1, 0, 2)
    width = 2 * feature_width // PIECES
    got, got_hot, all_hot = exchange(
        send.reshape(capacity, nz, nq, PIECES, width),
        send_hot.reshape(nz, nq, hot_slots, hot_width),
        own_hot,
        nz,
        nq,
    )
    shadow_gate, shadow_up, shadow_down = (
        spread(w_gate[0], "expert", hot_expert),
        spread(w_up[0], "expert", hot_expert),
        spread(w_down[0], "expert", hot_expert),
    )
    rows = got.reshape(capacity * 4 * experts, 2 * feature_width)
    cold_tokens, cold_grads = rows[:, :feature_width], rows[:, feature_width:]
    hidden, gate_grad, up_grad = expert_terms(
        cold_tokens, cold_grads, w_gate[0], w_up[0], w_down[0]
    )
    grad_gate = column_sum(cold_tokens, gate_grad).astype(jnp.bfloat16)
    grad_up = column_sum(cold_tokens, up_grad).astype(jnp.bfloat16)
    grad_down = column_sum(hidden, cold_grads).astype(jnp.bfloat16)
    hot_rows = all_hot.reshape(4 * hot_slots, 2 * feature_width)
    hot_hidden, hot_gate_grad, hot_up_grad = expert_terms(
        hot_rows[:, :feature_width], hot_rows[:, feature_width:],
        shadow_gate, shadow_up, shadow_down,
    )
    hot_terms = lax.all_gather(
        jnp.concatenate([hot_gate_grad, hot_up_grad, hot_hidden], axis=1),
        "expert", axis=0, tiled=True,
    )
    ff = w_gate.shape[2]
    sums = column_sum(got_hot.reshape(experts * 4 * hot_slots, hot_width), hot_terms)
    hot_grads = jnp.stack(
        [sums[:part, :ff], sums[:part, ff : 2 * ff], sums[part : 2 * part, 2 * ff :]], axis=1
    ).astype(jnp.bfloat16)[None]
    return (grad_gate[None], grad_up[None], grad_down[None], hot_grads)


def solution(mesh):
    placed = (
        P(("dp", "expert"), None),
        P(("dp", "expert"), None),
        P(("dp", "expert")),
        P(("dp", "expert")),
        P(),
        P("expert", None, "dp"),
        P("expert", None, "dp"),
        P("expert", "dp", None),
    )
    return jax.shard_map(
        on_device,
        mesh=mesh,
        in_specs=placed,
        out_specs=(
            P("expert", None, "dp"),
            P("expert", None, "dp"),
            P("expert", "dp", None),
            P(None, "expert", None, "dp"),
        ),
        check_vma=False,
    )
```

time: 429 us -> 349 us (0.81)
  blocking collectives: 141 us -> 0 us
  Pallas kernels: 0 us -> 139 us
  waiting for transfers between devices: 210 us -> 149 us
  matrix products: 28.5 us -> 23.4 us
    pallas_call x0 -> x1, Pallas kernels: none -> 139 us  [exchange(): pl.pallas_call(body, out_shape=(jax.ShapeDtypeStruct((slots, 4, nq, nz, p...]
    reduce_scatter x1 -> x0, waiting for transfers between devices: 133 us -> none  [on_device(): lax.psum_scatter(jnp.stack([gate_part, up_part, down_part], axis=1), 'exp...]
    all_to_all x2 -> x0, blocking collectives: 120 us -> none  [the longest x1 66.8 us: on_device(): lax.all_to_all(send_tokens, 'expert', split_axis=0, concat_axis=0, tiled=...]
    all_gather x2 -> x1, waiting for transfers between devices: 0.05 us -> 57 us  [on_device(): lax.all_gather(jnp.concatenate([hot_gate_grad, hot_up_grad, hot_hidden],...]
    all_gather x2 -> x0, blocking collectives: 20.6 us -> none  [the longest x1 11 us: on_device(): lax.all_gather(own_hot_grads, 'dp', axis=0, tiled=True)]
    psum x1, waiting for transfers between devices: 76.6 us -> 91.7 us  [spread(): return lax.psum(block, axis)]
    reshape x4 -> x2, local copies, waits for them, and re-layouts: 13.5 us -> 0.47 us  [the longest x1 0.23 us: on_device(): own_hot[:, :feature_width].reshape(hot_slots, experts, part)]
    unnamed x42 -> x22, local copies, waits for them, and re-layouts: 3.6 us -> 12.9 us
  transfers between devices with their start and end apart: 4 -> 2, of which waited for: 2 -> 2; matrix products, arithmetic and copies ran while one was open for 11% -> 8% of each run, Pallas kernels for 0% -> 40%
where the time goes in v1:
time: 349 us; the launch traced here: 348 us
  waiting for transfers between devices  149 us (43%)
  Pallas kernels  139 us (40%)
  matrix products  23.4 us (7%)
  between operations  14.9 us (4%)
  local copies, waits for them, and re-layouts  13.7 us (4%)
  other arithmetic  8.64 us (2%)
    pallas_call x1, Pallas kernels, exchange(): pl.pallas_call(body, out_shape=(jax.ShapeDtypeStruct((slots, 4, nq, nz, p...  139 us
    psum x1, waiting for transfers between devices, spread(): return lax.psum(block, axis)  91.7 us
    all_gather x1, waiting for transfers between devices, on_device(): lax.all_gather(jnp.concatenate([hot_gate_grad, hot_up_grad, hot_hidden],...  57 us
    unnamed x22, local copies, waits for them, and re-layouts  12.9 us
    dot_general x4, matrix products, column_sum(): lax.dot_general(left, right, CONTRACT_ROWS, preferred_element_type=jnp.fl...  11.9 us
  transfers between devices with their start and end apart: 2, of which 2 were waited for; matrix products, arithmetic and copies ran while one was open for 8% of the time, Pallas kernels for 40%

profile of v1, /device:TPU:1, one launch (start us, length us, event | category | flops | bytes accessed | tf_op | source)
XLA Modules:
  0.0 348.2 jit_solution(2487937594704586356)
XLA Ops:
  7.9 3.0 bitcast_select_fusion.2
  10.9 2.1 bitcast_select_fusion
  13.0 0.6 copy-done.7
  13.7 0.1 copy.14
  13.8 0.2 reduce-window.8
  14.1 0.1 fusion.28
  14.2 0.2 reduce_window_sum.18
  14.4 1.4 multiply_convert_fusion
  15.8 1.5 convolution_convert_fusion.1.refs_2_
  17.3 0.2 reshape.113
  17.6 0.2 reshape.114
  17.9 0.1 maximum_bitcast_fusion
  18.1 0.2 select_reduce_fusion
  18.3 2.0 convolution_convert_fusion
  20.3 0.5 copy.16
  20.9 138.8 %shard_map.111 = (bf16[3,4,8,8,8,896]{5,4,3,2,1,0:T(8,128)(2,1)S(1)}, bf16[8,8,4,8,128]{4,3,2,1,0:T(8,128)(2,1)S(1)}, bf16[4,8,7168]{2,1,0:T(8,128)(2,1)S(1)}) custom-call(bf16[3,8,8,8,896]{4,3,2,1,0:T(8,128)(2,1)S(1)} %bitcast.45, bf16[8,8,8,128]{3,2,1,0:T(8,128)(2,1)S(1)} %bitcast.49, bf16[8,7168]{1,0:T(8,128)(2,1)S(1)} %convolution_convert_fusion.1.refs_2_), custom_call_target="tpu_custom_call" | custom-call | bytes 300000000 | tf_op jit(solution)/shard_map/pallas_call | solution.py:191
  159.6 4.2 %copy-done = bf16[3,4,8,8,8,896]{5,4,3,2,1,0:T(8,128)(2,1)} copy-done((bf16[3,4,8,8,8,896]{5,4,3,2,1,0:T(8,128)(2,1)}, bf16[3,4,8,8,8,896]{5,4,3,2,1,0:T(8,128)(2,1)S(1)}, u32[]{:S(2)}) %copy-start) | copy-done | bytes 11010072
  163.8 91.7 %all-reduce.3.cloned.1.call-done = (bf16[3584,256]{1,0:T(8,128)(2,1)}, bf16[3584,256]{1,0:T(8,128)(2,1)}, bf16[256,3584]{1,0:T(8,128)(2,1)}) async-done(((bf16[3584,256]{1,0:T(8,128)(2,1)}, bf16[3584,256]{1,0:T(8,128)(2,1)}, bf16[256,3584]{1,0:T(8,128)(2,1)}), (bf16[3584,256]{1,0:T(8,128)(2,1)}, bf16[3584,256]{1,0:T(8,128)(2,1)}, bf16[256,3584]{1,0:T(8,128)(2,1)})) %all-reduce.3.cloned.1.call-update) | async-done | bytes 5505040 | tf_op jit(solution)/shard_map/psum | solution.py:15
  255.5 2.1 fusion.21
  257.6 0.6 fusion.17
  258.2 0.4 multiply_convert_fusion.9
  258.7 0.6 pad_maximum_fusion.4
  259.3 7.5 %copy.17 = bf16[96,8,8,896]{3,1,2,0:T(8,128)(2,1)S(1)} copy(bf16[96,8,8,896]{3,2,1,0:T(8,128)(2,1)} %bitcast.44) | data formatting | bytes 22020096
  266.9 1.6 fusion.8
  268.5 1.6 fusion.4
  270.1 1.6 fusion.10
  271.7 3.0 fusion.2
  274.7 3.2 fusion.1
  277.9 3.2 fusion
  281.2 57.0 %all-gather.2.cloned.1.call-done = bf16[2048,768]{1,0:T(8,128)(2,1)} async-done(((bf16[32,768]{1,0:T(8,128)(2,1)}), bf16[2048,768]{1,0:T(8,128)(2,1)}) %all-gather.2.cloned.1.call-update) | async-done | bytes 3145744 | tf_op jit(solution)/shard_map/all_gather | solution.py:281
  338.2 2.5 convolution_convert_fusion.5
  340.7 0.6 pad_maximum_fusion.3
  (31 shorter events, 0.6 us)
Async XLA Ops:
  7.2 248.4 %all-reduce.3.cloned.1.call-start = ((), (), s32[]{:S(2)}) async-start(), calls=%async_computation.1 | async-start | bytes 11010048 | tf_op jit(solution)/shard_map/psum | solution.py:15
  7.9 3.0 copy-start.4
  7.9 3.0 copy-start.5
  13.0 0.7 copy-start.7
  13.0 0.7 copy-start.8
  13.0 1.4 copy-start.9
  13.0 325.2 %all-gather.2.cloned.1.call-start = ((), (), s32[]{:S(2)}) async-start(), calls=%async_computation | async-start | bytes 3194880 | tf_op jit(solution)/shard_map/all_gather | solution.py:281
  159.6 4.2 %copy-start = (bf16[3,4,8,8,8,896]{5,4,3,2,1,0:T(8,128)(2,1)}, bf16[3,4,8,8,8,896]{5,4,3,2,1,0:T(8,128)(2,1)S(1)}, u32[]{:S(2)}) copy-start(bf16[3,4,8,8,8,896]{5,4,3,2,1,0:T(8,128)(2,1)S(1)} %get-tuple-element.7) | copy-start | bytes 33030148
  255.5 2.1 copy-start.3
  255.5 2.7 copy-start.2
  266.9 1.6 copy-start.1
  268.5 1.6 copy-start.6
Sparse Core Ops, SparseCore 0:
  13.1 242.3 all-reduce.2
  259.5 78.6 all-gather.1

commit v2 on v1

v2 whole, which is shorter than its diff:
```python
import jax
import jax.numpy as jnp
from jax import lax
from jax.experimental import pallas as pl
from jax.experimental.pallas import tpu as pltpu
from jax.sharding import PartitionSpec as P

CONTRACT_ROWS = (((0,), (0,)), ((), ()))
MESH = pl.DeviceIdType.MESH
PIECES = 8


def terms_of(pre_gate, pre_up, hidden_back):
    sigmoid_gate = jax.nn.sigmoid(pre_gate)
    activated = pre_gate * sigmoid_gate
    hidden = (activated * pre_up).astype(jnp.bfloat16)
    gate_grad = (
        hidden_back * pre_up * sigmoid_gate * (1.0 + pre_gate * (1.0 - sigmoid_gate))
    ).astype(jnp.bfloat16)
    up_grad = (hidden_back * activated).astype(jnp.bfloat16)
    return (hidden, gate_grad, up_grad)


def expert_terms(row_tokens, row_grads, gate_matrix, up_matrix, down_matrix):
    pre_gate = jnp.dot(row_tokens, gate_matrix, preferred_element_type=jnp.float32)
    pre_up = jnp.dot(row_tokens, up_matrix, preferred_element_type=jnp.float32)
    hidden_back = lax.dot_general(
        row_grads, down_matrix, (((1,), (1,)), ((), ())), preferred_element_type=jnp.float32
    )
    return terms_of(pre_gate, pre_up, hidden_back)


def column_sum(left, right):
    return lax.dot_general(left, right, CONTRACT_ROWS, preferred_element_type=jnp.float32)


def route_rows(selector, values):
    return jnp.dot(selector, values, preferred_element_type=jnp.float32).astype(jnp.bfloat16)


def exchange_kernel(nz, nx, nc, send, send_hot, hot_rows, hot_at, w_gate, w_up, w_down,
                    got, got_hot, hot_terms,
                    mid, mid_hot, pair_gu, pair_d, one_gu, one_d, row_gu, row_d,
                    two_gu, two_d, col_gu, col_d, three_gu, three_d, full_gu, full_d,
                    hot_in, part, parts, own_terms,
                    z_send, z_recv, q_send, q_recv, local_sem,
                    y_send, y_recv, f_send, f_recv,
                    c_send, c_recv, x_send, x_recv, w_send, w_recv, g_send, g_recv,
                    r_send, r_recv, v_send, v_recv, p_send, p_recv,
                    t_send, t_recv, u_send, u_recv, b_send, b_recv, own_sem):
    ny = 4
    nq = nx * nc
    chunks = send.shape[0]
    y = lax.axis_index("dp")
    e = lax.axis_index("expert")
    z = lax.div(e, nq)
    q = lax.rem(e, nq)
    x = lax.div(q, nc)
    c = lax.rem(q, nc)
    up = lax.rem(y + 1, ny)
    down = lax.rem(y + ny - 1, ny)
    twin = (y, z * nq + x * nc + (1 - c))
    half = w_gate.shape[0] // nc
    width = w_gate.shape[1]
    span = one_gu.shape[1] // 14 * 4
    z_rows = span // nz
    d_rows = width // nz

    def z_peer(k):
        return lax.rem(z + k, nz)

    def q_peer(k):
        return lax.rem(q + k, nq)

    def q_source(k):
        return lax.rem(q + nq - k, nq)

    def x_peer(k):
        return lax.rem(x + k, nx)

    def z_dev(k):
        return (y, z_peer(k) * nq + q)

    def q_dev(k):
        return (y, z * nq + q_peer(k))

    def x_dev(k):
        return (y, z * nq + x_peer(k) * nc + c)

    def remote(src, dst, send_sem, recv_sem, device):
        return pltpu.make_async_remote_copy(
            src_ref=src, dst_ref=dst, send_sem=send_sem, recv_sem=recv_sem,
            device_id=device, device_id_type=MESH)

    barrier = pltpu.get_barrier_semaphore()
    for k in range(1, nz):
        pl.semaphore_signal(barrier, inc=1, device_id=z_dev(k), device_id_type=MESH)
    for k in range(1, nq):
        pl.semaphore_signal(barrier, inc=1, device_id=q_dev(k), device_id_type=MESH)
    for k in range(1, ny):
        pl.semaphore_signal(barrier, inc=1, device_id=(lax.rem(y + k, ny), e), device_id_type=MESH)
    pl.semaphore_wait(barrier, nz - 1 + nq - 1 + ny - 1)

    def z_refs(s):
        if s < chunks:
            return send.at[s], mid.at[s]
        return send_hot, mid_hot

    def q_dst(s, who):
        if s < chunks:
            return got.at[s, y, who]
        return got_hot.at[:, who, y]

    def y_block(s, who, plane):
        if s < chunks:
            return got.at[s, plane, who]
        return got_hot.at[:, who, plane]

    def z_copy(s, k):
        src, dst = z_refs(s)
        return remote(src.at[z_peer(k)], dst.at[z], z_send.at[s, k - 1], z_recv.at[s, k - 1], z_dev(k))

    def z_own(s):
        src, dst = z_refs(s)
        return pltpu.make_async_copy(src.at[z], dst.at[z], local_sem.at[s, 0])

    def q_copy(s, k):
        _, src = z_refs(s)
        return remote(src.at[:, q_peer(k)], q_dst(s, q), q_send.at[s, k - 1], q_recv.at[s, k - 1], q_dev(k))

    def q_own(s):
        _, src = z_refs(s)
        return pltpu.make_async_copy(src.at[:, q], q_dst(s, q), local_sem.at[s, 1])

    def y_copy(s, k, way):
        block = y_block(s, q_source(k), y)
        return remote(block, block, y_send.at[s, k, way], y_recv.at[s, k, way],
                      (up if way == 0 else down, e))

    def f_copy(s, k):
        way = 0 if k < nq // 2 else 1
        block = y_block(s, q_source(k), down if way == 0 else up)
        return remote(block, block, f_send.at[s, k], f_recv.at[s, k],
                      (up if way == 0 else down, e))

    z_order = sorted(range(1, nz), key=lambda k: -min(k, nz - k))

    def start_z(s):
        z_own(s).start()
        for k in z_order:
            z_copy(s, k).start()

    def pass_on(s, k):
        way = 0 if k < nq // 2 else 1
        y_copy(s, k, way).wait_recv()
        f_copy(s, k).start()

    def run_chunk(s):
        z_own(s).wait()
        for k in z_order:
            z_copy(s, k).wait_recv()
        q_own(s).start()
        for k in range(1, nq):
            q_copy(s, k).start()
        for k in range(nq):
            if k == 0:
                q_own(s).wait()
            else:
                q_copy(s, k).wait_recv()
            y_copy(s, k, 0).start()
            y_copy(s, k, 1).start()
            if s > 0:
                pass_on(s - 1, k)

    def row_half(who):
        return pl.ds(pl.multiple_of(who * half, half), half)

    def c_copies(who):
        return (
            (w_gate.at[row_half(who), :], pair_gu.at[c, 0]),
            (w_up.at[row_half(who), :], pair_gu.at[c, 1]),
            (w_down.at[:, row_half(who)], pair_d.at[c]),
        )

    def c_copy(i):
        src, dst = c_copies(1 - c)[i]
        return remote(src, dst, c_send.at[i], c_recv.at[i], twin)

    def c_own(i):
        src, dst = c_copies(c)[i]
        return pltpu.make_async_copy(src, dst, own_sem.at[i])

    def x_span(who):
        first = who * 3 + lax.div(who, 2)
        return pl.ds(pl.multiple_of(first * (half // 14), half // 14), span)

    def x_pair(who):
        return (
            (one_gu.at[:, x_span(who), :], row_gu.at[x]),
            (one_d.at[:, x_span(who)], row_d.at[x]),
        )

    def x_copy(k, i):
        src, dst = x_pair(x_peer(k))[i]
        return remote(src, dst, x_send.at[k - 1, i], x_recv.at[k - 1, i], x_dev(k))

    def x_own(i):
        src, dst = x_pair(x)[i]
        return pltpu.make_async_copy(src, dst, own_sem.at[3 + i])

    def z_part(who):
        return pl.ds(pl.multiple_of(who * z_rows, z_rows), z_rows)

    def d_part(who):
        return pl.ds(pl.multiple_of(who * d_rows, d_rows), d_rows)

    def w_pair(who):
        return (
            (two_gu.at[:, z_part(who), :], col_gu.at[z]),
            (two_d.at[d_part(who), :], col_d.at[z]),
        )

    def w_copy(k, i):
        src, dst = w_pair(z_peer(k))[i]
        return remote(src, dst, w_send.at[k - 1, i], w_recv.at[k - 1, i], z_dev(k))

    def w_own(i):
        src, dst = w_pair(z)[i]
        return pltpu.make_async_copy(src, dst, own_sem.at[5 + i])

    g_pair = (
        (three_gu, full_gu.at[:, z_part(z), :]),
        (three_d, full_d.at[d_part(z), :]),
    )

    def g_copy(k, i):
        src, dst = g_pair[i]
        return remote(src, dst, g_send.at[k - 1, i], g_recv.at[k - 1, i], z_dev(k))

    def g_own(i):
        src, dst = g_pair[i]
        return pltpu.make_async_copy(src, dst, own_sem.at[7 + i])

    def r_copy(k):
        return remote(hot_rows.at[q_peer(k)], hot_in.at[y, q], r_send.at[k - 1], r_recv.at[k - 1], q_dev(k))

    r_own = pltpu.make_async_copy(hot_rows.at[q], hot_in.at[y, q], own_sem.at[9])

    def v_copy(k):
        return remote(hot_in.at[y], hot_in.at[y], v_send.at[k - 1], v_recv.at[k - 1],
                      (lax.rem(y + k, ny), e))

    def p_copy(k):
        return remote(part.at[:, q_peer(k)], parts.at[q], p_send.at[k - 1], p_recv.at[k - 1], q_dev(k))

    p_own = pltpu.make_async_copy(part.at[:, q], parts.at[q], own_sem.at[10])

    def t_copy(k):
        return remote(own_terms, hot_terms.at[z, x, c], t_send.at[k - 1], t_recv.at[k - 1], z_dev(k))

    t_own = pltpu.make_async_copy(own_terms, hot_terms.at[z, x, c], own_sem.at[11])

    def u_copy(k):
        block = hot_terms.at[:, x, c]
        return remote(block, block, u_send.at[k - 1], u_recv.at[k - 1], x_dev(k))

    def b_copy():
        block = hot_terms.at[:, :, c]
        return remote(block, block, b_send.at[0], b_recv.at[0], twin)

    hot_z = hot_at[0]
    hot_x = hot_at[1]
    hot_c = hot_at[2]

    for i in range(3):
        c_copy(i).start()
        c_own(i).start()
    r_own.start()
    for k in range(1, nq):
        r_copy(k).start()
    start_z(0)
    start_z(chunks)
    start_z(1)
    for i in range(3):
        c_own(i).wait()
        c_copy(i).wait_recv()

    tile = half // 14

    def keep_half(n, carry):
        rows = pl.ds(pl.multiple_of(n * tile, tile), tile)
        one_gu[0, rows, :] = pair_gu[hot_c, 0, rows, :]
        one_gu[1, rows, :] = pair_gu[hot_c, 1, rows, :]
        one_d[:, rows] = pair_d[hot_c, :, rows]
        return carry

    lax.fori_loop(0, 14, keep_half, 0)
    for i in range(2):
        x_own(i).start()
        for k in range(1, nx):
            x_copy(k, i).start()

    r_own.wait()
    for k in range(1, nq):
        r_copy(k).wait_recv()
    for k in range(1, ny):
        v_copy(k).start()

    run_chunk(0)

    for i in range(2):
        x_own(i).wait()
        for k in range(1, nx):
            x_copy(k, i).wait_recv()
    two_gu[...] = row_gu[hot_x]
    two_d[...] = row_d[hot_x]
    for i in range(2):
        w_own(i).start()
        for k in z_order:
            w_copy(k, i).start()
    start_z(2)

    run_chunk(1)

    for i in range(2):
        w_own(i).wait()
        for k in z_order:
            w_copy(k, i).wait_recv()
    three_gu[...] = col_gu[hot_z]
    three_d[...] = col_d[hot_z]
    for i in range(2):
        g_own(i).start()
        for k in z_order:
            g_copy(k, i).start()

    run_chunk(2)

    for k in range(1, ny):
        v_copy(k).wait_recv()
    for i in range(2):
        g_own(i).wait()
        for k in z_order:
            g_copy(k, i).wait_recv()
    rows = hot_in[...].astype(jnp.float32).reshape(ny * nq * 8, 2 * span).astype(jnp.bfloat16)
    row_tokens, row_grads = rows[:, :span], rows[:, span:]
    flat = (ny, nq, 8, width)
    part[:, :, :, 0:width] = jnp.dot(
        row_tokens, full_gu[0], preferred_element_type=jnp.float32).reshape(flat)
    part[:, :, :, width : 2 * width] = jnp.dot(
        row_tokens, full_gu[1], preferred_element_type=jnp.float32).reshape(flat)
    part[:, :, :, 2 * width :] = lax.dot_general(
        row_grads, full_d[...], (((1,), (1,)), ((), ())),
        preferred_element_type=jnp.float32).reshape(flat)
    p_own.start()
    for k in range(1, nq):
        p_copy(k).start()

    run_chunk(chunks)

    p_own.wait()
    for k in range(1, nq):
        p_copy(k).wait_recv()
    total = parts[0]
    for k in range(1, nq):
        total = total + parts[k]
    total = total.reshape(ny * 8, 3 * width)
    pre_gate, pre_up, hidden_back = (
        total[:, :width], total[:, width : 2 * width], total[:, 2 * width :])
    hidden, gate_grad, up_grad = terms_of(pre_gate, pre_up, hidden_back)
    own_terms[:, 0:width] = gate_grad
    own_terms[:, width : 2 * width] = up_grad
    own_terms[:, 2 * width :] = hidden
    t_own.start()
    for k in z_order:
        t_copy(k).start()

    for k in range(nq):
        pass_on(chunks, k)

    t_own.wait()
    for k in z_order:
        t_copy(k).wait_recv()
    for k in range(1, nx):
        u_copy(k).start()
    for k in range(1, nx):
        u_copy(k).wait_recv()
    b_copy().start()
    b_copy().wait()

    for i in range(3):
        c_copy(i).wait_send()
    for k in range(1, nx):
        u_copy(k).wait_send()
        for i in range(2):
            x_copy(k, i).wait_send()
    for k in range(1, nz):
        t_copy(k).wait_send()
        for i in range(2):
            w_copy(k, i).wait_send()
            g_copy(k, i).wait_send()
    for k in range(1, ny):
        v_copy(k).wait_send()
    for k in range(1, nq):
        r_copy(k).wait_send()
        p_copy(k).wait_send()
    for s in range(chunks + 1):
        for k in range(1, nz):
            z_copy(s, k).wait_send()
        for k in range(1, nq):
            q_copy(s, k).wait_send()
        for k in range(nq):
            y_copy(s, k, 0).wait_send()
            y_copy(s, k, 1).wait_send()
            y_copy(s, k, 1 if k < nq // 2 else 0).wait_recv()
            f_copy(s, k).wait()


def exchange(send, send_hot, hot_rows, hot_at, w_gate, w_up, w_down, nz, nx, nc):
    slots, _, nq, pieces, wide = send.shape
    hot_slots, hot_width = send_hot.shape[-2:]
    bf16, f32 = jnp.bfloat16, jnp.float32
    steps = slots + 1
    dma = pltpu.SemaphoreType.DMA
    rows, width = w_gate.shape
    half = rows // nc
    span = half // 14 * 4

    def body(*refs):
        exchange_kernel(nz, nx, nc, *refs)

    hbm = pl.BlockSpec(memory_space=pl.ANY)
    vmem = pl.BlockSpec(memory_space=pltpu.VMEM)
    smem = pl.BlockSpec(memory_space=pltpu.SMEM)
    return pl.pallas_call(
        body,
        out_shape=(
            jax.ShapeDtypeStruct((slots, 4, nq, nz, pieces, wide), bf16),
            jax.ShapeDtypeStruct((nz, nq, 4, hot_slots, hot_width), bf16),
            jax.ShapeDtypeStruct((nz, nx, nc, 4 * hot_slots, 3 * width), bf16),
        ),
        in_specs=[hbm, hbm, vmem, smem, hbm, hbm, hbm],
        out_specs=(hbm, hbm, hbm),
        scratch_shapes=[
            pltpu.VMEM((slots, nz, nq, pieces, wide), bf16),
            pltpu.VMEM((nz, nq, hot_slots, hot_width), bf16),
            pltpu.VMEM((nc, 2, half, width), bf16),
            pltpu.VMEM((nc, width, half), bf16),
            pltpu.VMEM((2, half, width), bf16),
            pltpu.VMEM((width, half), bf16),
            pltpu.VMEM((nx, 2, span, width), bf16),
            pltpu.VMEM((nx, width, span), bf16),
            pltpu.VMEM((2, span, width), bf16),
            pltpu.VMEM((width, span), bf16),
            pltpu.VMEM((nz, 2, span // nz, width), bf16),
            pltpu.VMEM((nz, width // nz, span), bf16),
            pltpu.VMEM((2, span // nz, width), bf16),
            pltpu.VMEM((width // nz, span), bf16),
            pltpu.VMEM((2, span, width), bf16),
            pltpu.VMEM((width, span), bf16),
            pltpu.VMEM((4, nq, hot_slots, 2 * span), bf16),
            pltpu.VMEM((4, nq, hot_slots, 3 * width), f32),
            pltpu.VMEM((nq, 4, hot_slots, 3 * width), f32),
            pltpu.VMEM((4 * hot_slots, 3 * width), bf16),
            dma((steps, nz - 1)),
            dma((steps, nz - 1)),
            dma((steps, nq - 1)),
            dma((steps, nq - 1)),
            dma((steps, 2)),
            dma((steps, nq, 2)),
            dma((steps, nq, 2)),
            dma((steps, nq)),
            dma((steps, nq)),
            dma((3,)),
            dma((3,)),
            dma((nx - 1, 2)),
            dma((nx - 1, 2)),
            dma((nz - 1, 2)),
            dma((nz - 1, 2)),
            dma((nz - 1, 2)),
            dma((nz - 1, 2)),
            dma((nq - 1,)),
            dma((nq - 1,)),
            dma((3,)),
            dma((3,)),
            dma((nq - 1,)),
            dma((nq - 1,)),
            dma((nz - 1,)),
            dma((nz - 1,)),
            dma((nx - 1,)),
            dma((nx - 1,)),
            dma((1,)),
            dma((1,)),
            dma((12,)),
        ],
        compiler_params=pltpu.CompilerParams(
            collective_id=0, has_side_effects=True, vmem_limit_bytes=40 * 1024 * 1024
        ),
        cost_estimate=pl.CostEstimate(flops=0, bytes_accessed=300_000_000, transcendentals=0),
    )(send, send_hot, hot_rows, hot_at, w_gate, w_up, w_down)


def on_device(tokens, cotangent, gate_scale, expert_index, hot_index, w_gate, w_up, w_down):
    tok_rows, feature_width = tokens.shape
    experts = lax.axis_size("expert")
    nx, nc = 4, 2
    nq = nx * nc
    nz = experts // nq
    capacity = 3 * tok_rows // (2 * experts)
    hot_slots = 8
    hot_expert = hot_index[0]
    route_grad = (gate_scale[:, None] * cotangent.astype(jnp.float32)).astype(jnp.bfloat16)
    both = jnp.concatenate([tokens, route_grad], axis=1)
    is_hot = expert_index == hot_expert
    not_hot = jnp.logical_not(is_hot)
    owners = lax.broadcasted_iota(jnp.int32, (tok_rows, experts), 1)
    member = ((expert_index[:, None] == owners) & not_hot[:, None]).astype(jnp.int32)
    bucket_place = jnp.sum((jnp.cumsum(member, axis=0) - 1) * member, axis=1)
    slot_index = bucket_place * experts + expert_index
    slot_grid = lax.broadcasted_iota(jnp.int32, (experts * capacity, tok_rows), 0)
    cold_map = ((slot_grid == slot_index[None, :]) & not_hot[None, :]).astype(jnp.bfloat16)
    hot_place = jnp.cumsum(is_hot.astype(jnp.int32)) - 1
    hot_grid = lax.broadcasted_iota(jnp.int32, (hot_slots, tok_rows), 0)
    hot_map = ((hot_grid == hot_place[None, :]) & is_hot[None, :]).astype(jnp.bfloat16)
    send = route_rows(cold_map, both)
    own_hot = route_rows(hot_map, both)
    part = feature_width // experts
    hot_width = -(-2 * part // 128) * 128
    send_hot = jnp.concatenate(
        [
            own_hot[:, :feature_width].reshape(hot_slots, experts, part),
            own_hot[:, feature_width:].reshape(hot_slots, experts, part),
            jnp.zeros((hot_slots, experts, hot_width - 2 * part), jnp.bfloat16),
        ],
        axis=2,
    ).transpose(1, 0, 2)
    width = 2 * feature_width // PIECES
    half = feature_width // nc
    tile = half // 14
    hot_rows = jnp.stack(
        [
            jnp.concatenate(
                [
                    jnp.concatenate(
                        [
                            own_hot[:, at : at + (3 + x % 2) * tile],
                            jnp.zeros((hot_slots, (1 - x % 2) * tile), jnp.bfloat16),
                        ],
                        axis=1,
                    )
                    for at in (
                        c * half + (7 * x // 2) * tile,
                        feature_width + c * half + (7 * x // 2) * tile,
                    )
                ],
                axis=1,
            )
            for x in range(nx)
            for c in range(nc)
        ]
    )
    hot_at = jnp.stack([hot_expert // nq, hot_expert % nq // nc, hot_expert % nc])
    got, got_hot, hot_terms = exchange(
        send.reshape(capacity, nz, nq, PIECES, width),
        send_hot.reshape(nz, nq, hot_slots, hot_width),
        hot_rows,
        hot_at,
        w_gate[0],
        w_up[0],
        w_down[0],
        nz,
        nx,
        nc,
    )
    rows = got.reshape(capacity * 4 * experts, 2 * feature_width)
    cold_tokens, cold_grads = rows[:, :feature_width], rows[:, feature_width:]
    hidden, gate_grad, up_grad = expert_terms(
        cold_tokens, cold_grads, w_gate[0], w_up[0], w_down[0]
    )
    grad_gate = column_sum(cold_tokens, gate_grad).astype(jnp.bfloat16)
    grad_up = column_sum(cold_tokens, up_grad).astype(jnp.bfloat16)
    grad_down = column_sum(hidden, cold_grads).astype(jnp.bfloat16)
    ff = w_gate.shape[2]
    hot_total = experts * 4 * hot_slots
    sums = column_sum(
        got_hot.reshape(hot_total, hot_width), hot_terms.reshape(hot_total, 3 * ff)
    )
    hot_grads = jnp.stack(
        [sums[:part, :ff], sums[:part, ff : 2 * ff], sums[part : 2 * part, 2 * ff :]], axis=1
    ).astype(jnp.bfloat16)[None]
    return (grad_gate[None], grad_up[None], grad_down[None], hot_grads)


def solution(mesh):
    placed = (
        P(("dp", "expert"), None),
        P(("dp", "expert"), None),
        P(("dp", "expert")),
        P(("dp", "expert")),
        P(),
        P("expert", None, "dp"),
        P("expert", None, "dp"),
        P("expert", "dp", None),
    )
    return jax.shard_map(
        on_device,
        mesh=mesh,
        in_specs=placed,
        out_specs=(
            P("expert", None, "dp"),
            P("expert", None, "dp"),
            P("expert", "dp", None),
            P(None, "expert", None, "dp"),
        ),
        check_vma=False,
    )
```

time: 349 us -> 206 us (0.59)
  waiting for transfers between devices: 149 us -> 0 us
  Pallas kernels: 139 us -> 172 us
  between operations: 14.9 us -> 1.11 us
  matrix products: 23.4 us -> 17.4 us
  other arithmetic: 8.64 us -> 4.4 us
    psum x1 -> x0, waiting for transfers between devices: 91.7 us -> none  [spread(): return lax.psum(block, axis)]
    all_gather x1 -> x0, waiting for transfers between devices: 57 us -> none  [on_device(): lax.all_gather(jnp.concatenate([hot_gate_grad, hot_up_grad, hot_hidden],...]
    pallas_call x1, Pallas kernels: 139 us -> 172 us  [exchange(): pl.pallas_call(body, out_shape=(jax.ShapeDtypeStruct((slots, 4, nq, nz, p...]
    select_n x2 -> x0, other arithmetic: 5.07 us -> none  [spread(): jnp.where(lax.axis_index(axis) == source, block, jnp.zeros_like(block))]
    unnamed x22 -> x14, local copies, waits for them, and re-layouts: 12.9 us -> 10.1 us
  transfers between devices with their start and end apart: 2 -> 0, of which waited for: 2 -> 0; matrix products, arithmetic and copies ran while one was open for 8% -> 0% of each run, Pallas kernels for 40% -> 0%
where the time goes in v2:
time: 206 us
  Pallas kernels  172 us (83%)
  matrix products  17.4 us (8%)
  local copies, waits for them, and re-layouts  10.9 us (5%)
  other arithmetic  4.4 us (2%)
    pallas_call x1, Pallas kernels, exchange(): pl.pallas_call(body, out_shape=(jax.ShapeDtypeStruct((slots, 4, nq, nz, p...  172 us
    dot_general x4, matrix products, column_sum(): lax.dot_general(left, right, CONTRACT_ROWS, preferred_element_type=jnp.fl...  10.2 us
    unnamed x14, local copies, waits for them, and re-layouts  10.1 us

profile of v2, /device:TPU:1, one launch (start us, length us, event | category | flops | bytes accessed | tf_op | source)
XLA Modules:
  0.0 205.5 jit_solution(3862066859467102691)
XLA Ops:
  0.7 0.0 copy-start.3
  0.7 1.4 convert_bitcast_fusion
  2.1 0.1 copy.14
  2.2 0.2 reduce-window.8
  2.3 0.1 add_reduce_fusion
  2.4 1.4 multiply_convert_fusion
  3.9 1.5 convolution_convert_fusion.1
  5.7 0.1 pad_add_fusion.refs_3_
  5.8 0.2 reshape.113
  6.0 0.2 reshape.114
  6.3 0.1 pad.32.clone
  6.4 0.1 maximum_bitcast_fusion
  6.5 0.1 copy.15
  6.6 0.1 fusion.19
  6.7 0.2 reduce_window_sum.18
  6.9 0.2 select_reduce_fusion
  7.1 0.9 convolution_convert_fusion
  8.0 0.0 copy-start.2
  8.0 0.5 copy.16
  8.5 0.9 copy-done
  9.5 0.6 copy-done.1
  10.0 0.6 copy-done.2
  10.6 171.8 %shard_map.111 = (bf16[3,4,8,8,8,896]{5,4,3,2,1,0:T(8,128)(2,1)}, bf16[8,8,4,8,128]{4,3,2,1,0:T(8,128)(2,1)S(1)}, bf16[8,4,2,32,768]{4,3,2,1,0:T(8,128)(2,1)S(1)}) custom-call(bf16[3,8,8,8,896]{4,3,2,1,0:T(8,128)(2,1)S(1)} %bitcast.73, bf16[8,8,8,128]{3,2,1,0:T(8,128)(2,1)S(1)} %bitcast.78, ...), custom_call_target="tpu_custom_call" | custom-call | bytes 300000000 | tf_op jit(solution)/shard_map/pallas_call | solution.py:434
  182.4 0.6 convolution_convert_fusion.5
  183.0 0.6 pad_maximum_fusion.3
  183.7 7.5 %copy.17 = bf16[96,8,8,896]{3,1,2,0:T(8,128)(2,1)S(1)} copy(bf16[96,8,8,896]{3,2,1,0:T(8,128)(2,1)} %bitcast.81) | data formatting | bytes 22020096
  191.2 1.6 fusion.10
  192.8 1.6 fusion.8
  194.4 3.0 %fusion.2 = bf16[1,256,3584]{2,1,0:T(8,128)(2,1)} fusion(bf16[768,7168]{1,0:T(8,128)(2,1)S(1)} %bitcast.84, f32[768,256]{1,0:T(8,128)S(1)} %fusion.10, f32[768,256]{1,0:T(8,128)S(1)} %fusion.8), kind=kOutput, calls=%fused_computation.7 | convolution fusion | flops 1411383296 | bytes 8912896 | tf_op jit(solution)/shard_map/dot_general | solution.py:34
  197.4 1.6 fusion.4
  199.0 3.2 %fusion.1 = bf16[1,3584,256]{2,1,0:T(8,128)(2,1)} fusion(bf16[768,7168]{1,0:T(8,128)(2,1)S(1)} %bitcast.86, f32[768,256]{1,0:T(8,128)S(1)} %fusion.4, f32[768,256]{1,0:T(8,128)S(1)} %fusion.8), kind=kOutput, calls=%fused_computation.6 | convolution fusion | flops 1411383296 | bytes 8912896 | tf_op jit(solution)/shard_map/dot_general | solution.py:34
  202.3 3.3 %fusion = bf16[1,3584,256]{2,1,0:T(8,128)(2,1)} fusion(bf16[768,7168]{1,0:T(8,128)(2,1)S(1)} %bitcast.87, f32[768,256]{1,0:T(8,128)S(1)} %fusion.8, f32[768,256]{1,0:T(8,128)S(1)} %fusion.4, f32[768,256]{1,0:T(8,128)S(1)} %fusion.10), kind=kOutput, calls=%fused_computation.5 | convolution fusion | flops 1412169728 | bytes 9699328 | tf_op jit(solution)/shard_map/dot_general | solution.py:34
  (23 shorter events, 0.1 us)
Async XLA Ops:
  0.6 4.9 %copy-start.5 = (s32[64]{0:T(128)S(1)}, s32[64]{0:T(128)}, u32[]{:S(2)}) copy-start(s32[64]{0:T(128)} %param.12) | copy-start | bytes 772
  0.6 6.0 %copy-start.4 = (s32[128]{0:T(128)S(1)}, s32[128]{0:T(128)}, u32[]{:S(2)}) copy-start(s32[128]{0:T(128)} %param.11) | copy-start | bytes 1540
  0.7 6.4 %copy-start.3 = (bf16[128,3584]{1,0:T(8,128)(2,1)S(1)}, bf16[128,3584]{1,0:T(8,128)(2,1)}, u32[]{:S(2)}) copy-start(bf16[128,3584]{1,0:T(8,128)(2,1)} %param.8) | copy-start | bytes 2752516
  8.0 1.5 copy-start
  8.0 2.0 copy-start.1
  8.0 2.6 %copy-start.2 = (bf16[1,256,3584]{2,1,0:T(8,128)(2,1)S(1)}, bf16[1,256,3584]{2,1,0:T(8,128)(2,1)}, u32[]{:S(2)}) copy-start(bf16[1,256,3584]{2,1,0:T(8,128)(2,1)} %param.15) | copy-start | bytes 5505028

commit v3 on v2

--- a/solution.py
+++ b/solution.py
@@ -21,15 +21,6 @@
     return (hidden, gate_grad, up_grad)
 
 
-def expert_terms(row_tokens, row_grads, gate_matrix, up_matrix, down_matrix):
-    pre_gate = jnp.dot(row_tokens, gate_matrix, preferred_element_type=jnp.float32)
-    pre_up = jnp.dot(row_tokens, up_matrix, preferred_element_type=jnp.float32)
-    hidden_back = lax.dot_general(
-        row_grads, down_matrix, (((1,), (1,)), ((), ())), preferred_element_type=jnp.float32
-    )
-    return terms_of(pre_gate, pre_up, hidden_back)
-
-
 def column_sum(left, right):
     return lax.dot_general(left, right, CONTRACT_ROWS, preferred_element_type=jnp.float32)
 
@@ -40,7 +31,7 @@
 
 def exchange_kernel(nz, nx, nc, send, send_hot, hot_rows, hot_at, w_gate, w_up, w_down,
                     got, got_hot, hot_terms,
-                    mid, mid_hot, pair_gu, pair_d, one_gu, one_d, row_gu, row_d,
+                    mid, mid_hot, turned, pair_gu, pair_d, one_gu, one_d, row_gu, row_d,
                     two_gu, two_d, col_gu, col_d, three_gu, three_d, full_gu, full_d,
                     hot_in, part, parts, own_terms,
                     z_send, z_recv, q_send, q_recv, local_sem,
@@ -51,6 +42,8 @@
     ny = 4
     nq = nx * nc
     chunks = send.shape[0]
+    pieces = send.shape[3]
+    group = 4
     y = lax.axis_index("dp")
     e = lax.axis_index("expert")
     z = lax.div(e, nq)
@@ -108,12 +101,12 @@
 
     def q_dst(s, who):
         if s < chunks:
-            return got.at[s, y, who]
+            return got.at[:, (s * ny + y) * nq + who]
         return got_hot.at[:, who, y]
 
     def y_block(s, who, plane):
         if s < chunks:
-            return got.at[s, plane, who]
+            return got.at[:, (s * ny + plane) * nq + who]
         return got_hot.at[:, who, plane]
 
     def z_copy(s, k):
@@ -124,13 +117,16 @@
         src, dst = z_refs(s)
         return pltpu.make_async_copy(src.at[z], dst.at[z], local_sem.at[s, 0])
 
+    def q_src(s, who):
+        if s < chunks:
+            return turned.at[s, who]
+        return mid_hot.at[:, who]
+
     def q_copy(s, k):
-        _, src = z_refs(s)
-        return remote(src.at[:, q_peer(k)], q_dst(s, q), q_send.at[s, k - 1], q_recv.at[s, k - 1], q_dev(k))
+        return remote(q_src(s, q_peer(k)), q_dst(s, q), q_send.at[s, k - 1], q_recv.at[s, k - 1], q_dev(k))
 
     def q_own(s):
-        _, src = z_refs(s)
-        return pltpu.make_async_copy(src.at[:, q], q_dst(s, q), local_sem.at[s, 1])
+        return pltpu.make_async_copy(q_src(s, q), q_dst(s, q), local_sem.at[s, 1])
 
     def y_copy(s, k, way):
         block = y_block(s, q_source(k), y)
@@ -155,10 +151,30 @@
         y_copy(s, k, way).wait_recv()
         f_copy(s, k).start()
 
-    def run_chunk(s):
+    block_rows = nz * group * pieces
+    to_row = lax.broadcasted_iota(jnp.int32, (block_rows, block_rows), 0)
+    from_row = lax.broadcasted_iota(jnp.int32, (block_rows, block_rows), 1)
+    wanted = (
+        (to_row % nz) * (group * pieces)
+        + (to_row // (pieces * nz)) * pieces
+        + (to_row // nz) % pieces
+    )
+    turn_map = jnp.where(from_row == wanted, 1.0, 0.0).astype(jnp.bfloat16)
+
+    def turn(s):
+        for g in range(nq // group):
+            block = mid[s, :, g * group : (g + 1) * group].astype(jnp.float32)
+            block = block.reshape(block_rows, block.shape[-1]).astype(jnp.bfloat16)
+            moved = jnp.dot(turn_map, block, preferred_element_type=jnp.float32)
+            turned[s, g * group : (g + 1) * group] = moved.reshape(
+                group, pieces, nz, moved.shape[-1]).astype(jnp.bfloat16)
+
+    def run_chunk(s, passing=True):
         z_own(s).wait()
         for k in z_order:
             z_copy(s, k).wait_recv()
+        if s < chunks:
+            turn(s)
         q_own(s).start()
         for k in range(1, nq):
             q_copy(s, k).start()
@@ -169,7 +185,7 @@
                 q_copy(s, k).wait_recv()
             y_copy(s, k, 0).start()
             y_copy(s, k, 1).start()
-            if s > 0:
+            if s > 0 and passing:
                 pass_on(s - 1, k)
 
     def row_half(who):
@@ -281,6 +297,7 @@
     start_z(0)
     start_z(chunks)
     start_z(1)
+    start_z(2)
     for i in range(3):
         c_own(i).wait()
         c_copy(i).wait_recv()
@@ -318,7 +335,6 @@
         w_own(i).start()
         for k in z_order:
             w_copy(k, i).start()
-    start_z(2)
 
     run_chunk(1)
 
@@ -355,7 +371,7 @@
     for k in range(1, nq):
         p_copy(k).start()
 
-    run_chunk(chunks)
+    run_chunk(chunks, False)
 
     p_own.wait()
     for k in range(1, nq):
@@ -375,13 +391,14 @@
         t_copy(k).start()
 
     for k in range(nq):
-        pass_on(chunks, k)
-
+        pass_on(2, k)
     t_own.wait()
     for k in z_order:
         t_copy(k).wait_recv()
     for k in range(1, nx):
         u_copy(k).start()
+    for k in range(nq):
+        pass_on(chunks, k)
     for k in range(1, nx):
         u_copy(k).wait_recv()
     b_copy().start()
@@ -434,7 +451,7 @@
     return pl.pallas_call(
         body,
         out_shape=(
-            jax.ShapeDtypeStruct((slots, 4, nq, nz, pieces, wide), bf16),
+            jax.ShapeDtypeStruct((pieces, slots * 4 * nq, nz, wide), bf16),
             jax.ShapeDtypeStruct((nz, nq, 4, hot_slots, hot_width), bf16),
             jax.ShapeDtypeStruct((nz, nx, nc, 4 * hot_slots, 3 * width), bf16),
         ),
@@ -443,6 +460,7 @@
         scratch_shapes=[
             pltpu.VMEM((slots, nz, nq, pieces, wide), bf16),
             pltpu.VMEM((nz, nq, hot_slots, hot_width), bf16),
+            pltpu.VMEM((slots, nq, pieces, nz, wide), bf16),
             pltpu.VMEM((nc, 2, half, width), bf16),
             pltpu.VMEM((nc, width, half), bf16),
             pltpu.VMEM((2, half, width), bf16),
@@ -571,14 +589,37 @@
         nx,
         nc,
     )
-    rows = got.reshape(capacity * 4 * experts, 2 * feature_width)
-    cold_tokens, cold_grads = rows[:, :feature_width], rows[:, feature_width:]
-    hidden, gate_grad, up_grad = expert_terms(
-        cold_tokens, cold_grads, w_gate[0], w_up[0], w_down[0]
-    )
-    grad_gate = column_sum(cold_tokens, gate_grad).astype(jnp.bfloat16)
-    grad_up = column_sum(cold_tokens, up_grad).astype(jnp.bfloat16)
-    grad_down = column_sum(hidden, cold_grads).astype(jnp.bfloat16)
+    rows = got.reshape(PIECES, capacity * 4 * experts, width)
+    cold_tokens, cold_grads = rows[: PIECES // 2], rows[PIECES // 2 :]
+    f32 = jnp.float32
+    pre_gate = sum(
+        jnp.dot(cold_tokens[n], w_gate[0, n * width : (n + 1) * width], preferred_element_type=f32)
+        for n in range(PIECES // 2)
+    )
+    pre_up = sum(
+        jnp.dot(cold_tokens[n], w_up[0, n * width : (n + 1) * width], preferred_element_type=f32)
+        for n in range(PIECES // 2)
+    )
+    hidden_back = sum(
+        lax.dot_general(
+            cold_grads[n],
+            w_down[0, :, n * width : (n + 1) * width],
+            (((1,), (1,)), ((), ())),
+            preferred_element_type=f32,
+        )
+        for n in range(PIECES // 2)
+    )
+    hidden, gate_grad, up_grad = terms_of(pre_gate, pre_up, hidden_back)
+    grad_gate = lax.dot_general(
+        cold_tokens, gate_grad, (((1,), (0,)), ((), ())), preferred_element_type=f32
+    ).astype(jnp.bfloat16).reshape(feature_width, -1)
+    grad_up = lax.dot_general(
+        cold_tokens, up_grad, (((1,), (0,)), ((), ())), preferred_element_type=f32
+    ).astype(jnp.bfloat16).reshape(feature_width, -1)
+    grad_down = jnp.concatenate(
+        [column_sum(hidden, cold_grads[n]).astype(jnp.bfloat16) for n in range(PIECES // 2)],
+        axis=1,
+    )
     ff = w_gate.shape[2]
     hot_total = experts * 4 * hot_slots
     sums = column_sum(

time: 206 us -> 198 us (0.961)
  Pallas kernels: 172 us -> 161 us
  local copies, waits for them, and re-layouts: 10.9 us -> 3.38 us
  matrix products: 17.4 us -> 21.9 us
  other arithmetic: 4.4 us -> 7.65 us
  between operations: 1.11 us -> 3.7 us
    dot_general x3 -> x14, matrix products: 4.83 us -> 17.7 us  [the longest x4 6.9 us: on_device(): jnp.dot(cold_tokens[n], w_gate[0, n * width:(n + 1) * width], preferred_e...]
    pallas_call x1, Pallas kernels: 172 us -> 161 us  [exchange(): pl.pallas_call(body, out_shape=(jax.ShapeDtypeStruct((pieces, slots * 4 *...]
    unnamed x14 -> x11, local copies, waits for them, and re-layouts: 10.1 us -> 2.59 us
    dot_general x4 -> x5, matrix products: 10.2 us -> 3.02 us  [column_sum(): lax.dot_general(left, right, CONTRACT_ROWS, preferred_element_type=jnp.fl...]
where the time goes in v3:
time: 198 us
  Pallas kernels  161 us (81%)
  matrix products  21.9 us (11%)
  other arithmetic  7.65 us (4%)
  between operations  3.7 us (2%)
  local copies, waits for them, and re-layouts  3.38 us (2%)
    pallas_call x1, Pallas kernels, exchange(): pl.pallas_call(body, out_shape=(jax.ShapeDtypeStruct((pieces, slots * 4 *...  161 us
    dot_general x4, matrix products, on_device(): jnp.dot(cold_tokens[n], w_gate[0, n * width:(n + 1) * width], preferred_e...  6.9 us

profile of v3, /device:TPU:1, one launch (start us, length us, event | category | flops | bytes accessed | tf_op | source)
XLA Modules:
  0.0 197.8 jit_solution(11653883436835477097)
XLA Ops:
  3.5 1.3 convert_bitcast_fusion
  5.2 0.8 fusion.131
  6.2 0.8 select_reduce_fusion
  7.0 0.7 multiply_add_fusion
  7.7 1.4 multiply_convert_fusion
  10.3 0.9 convolution_convert_fusion
  11.2 0.5 copy.22
  11.7 0.9 copy-done
  12.6 0.6 copy-done.1
  13.2 0.6 copy-done.2
  13.8 161.1 %shard_map.111 = (bf16[8,96,8,896]{3,2,1,0:T(8,128)(2,1)}, bf16[8,8,4,8,128]{4,3,2,1,0:T(8,128)(2,1)S(1)}, bf16[8,4,2,32,768]{4,3,2,1,0:T(8,128)(2,1)S(1)}) custom-call(bf16[3,8,8,8,896]{4,3,2,1,0:T(8,128)(2,1)S(1)} %bitcast.187, bf16[8,8,8,128]{3,2,1,0:T(8,128)(2,1)S(1)} %bitcast.192, bf16[8,8,1024]{2,1,0:T(8,128)(2,1)S(1)} %constant_dynamic-update-slice_fusion.refs_2_, ...), custom_call_target="tpu_custom_call" | custom-call | bytes 300000000 | tf_op jit(solution)/shard_map/pallas_call | solution.py:451
  174.9 0.6 convolution_convert_fusion.2
  175.6 0.6 pad_maximum_fusion.3
  176.2 2.5 %fusion.20 = f32[768,256]{1,0:T(8,128)S(1)} fusion(bf16[8,96,8,896]{3,2,1,0:T(8,128)(2,1)} %get-tuple-element.7, bf16[1,3584,256]{2,1,0:T(8,128)(2,1)S(1)} %copy-done), kind=kOutput, calls=%fused_computation.21 | convolution fusion | flops 352321536 | bytes 2621440 | tf_op jit(solution)/shard_map/dot_general | solution.py:596
  178.7 1.9 fusion.56
  180.6 1.9 fusion.62
  182.6 0.6 fusion.68
  183.1 0.6 fusion.22
  183.7 0.6 fusion.53
  184.3 0.6 fusion.59
  184.9 0.6 multiply_convert_fusion.1
  185.5 0.6 fusion.80
  186.1 0.6 fusion.77
  186.7 0.6 fusion.74
  187.3 0.6 fusion.71
  187.9 1.4 maximum_bitcast_fusion
  189.3 0.6 fusion.38
  189.9 0.6 fusion.44
  190.5 0.6 fusion.47
  191.1 0.6 fusion.50
  191.7 3.1 %fusion.6 = bf16[4,896,256]{2,1,0:T(8,128)(2,1)} fusion(bf16[8,96,8,896]{3,2,1,0:T(8,128)(2,1)S(1)} %copy-done.3, f32[768,256]{1,0:T(8,128)S(1)} %fusion.68, f32[768,256]{1,0:T(8,128)S(1)} %fusion.50, f32[768,256]{1,0:T(8,128)S(1)} %get-tuple-element.34), kind=kOutput, calls=%fused_computation.11 | convolution fusion | flops 1412169728 | bytes 9699328 | tf_op jit(solution)/shard_map/dot_general | solution.py:613
  194.8 3.0 %fusion.9 = bf16[4,896,256]{2,1,0:T(8,128)(2,1)} fusion(bf16[8,96,8,896]{3,2,1,0:T(8,128)(2,1)S(1)} %copy-done.3, f32[768,256]{1,0:T(8,128)S(1)} %fusion.50, f32[768,256]{1,0:T(8,128)S(1)} %fusion.68), kind=kOutput, calls=%fused_computation.12 | convolution fusion | flops 1411383296 | bytes 8912896 | tf_op jit(solution)/shard_map/dot_general | solution.py:616
  (33 shorter events, 1.8 us)
Async XLA Ops:
  0.6 8.4 %copy-start.4 = (bf16[128,3584]{1,0:T(8,128)(2,1)S(1)}, bf16[128,3584]{1,0:T(8,128)(2,1)}, u32[]{:S(2)}) copy-start(bf16[128,3584]{1,0:T(8,128)(2,1)} %param.8) | copy-start | bytes 2752516
  11.1 1.5 copy-start
  11.2 2.0 %copy-start.1 = (bf16[1,256,3584]{2,1,0:T(8,128)(2,1)S(1)}, bf16[1,256,3584]{2,1,0:T(8,128)(2,1)}, u32[]{:S(2)}) copy-start(bf16[1,256,3584]{2,1,0:T(8,128)(2,1)} %param.15) | copy-start | bytes 5505028
  11.2 2.6 %copy-start.2 = (bf16[1,3584,256]{2,1,0:T(8,128)(2,1)S(1)}, bf16[1,3584,256]{2,1,0:T(8,128)(2,1)}, u32[]{:S(2)}) copy-start(bf16[1,3584,256]{2,1,0:T(8,128)(2,1)} %param.14) | copy-start | bytes 5505028
  174.9 7.7 %copy-start.3 = (bf16[8,96,8,896]{3,2,1,0:T(8,128)(2,1)S(1)}, bf16[8,96,8,896]{3,2,1,0:T(8,128)(2,1)}, u32[]{:S(2)}) copy-start(bf16[8,96,8,896]{3,2,1,0:T(8,128)(2,1)} %get-tuple-element.7) | copy-start | bytes 33030148

commit v4 on v3

--- a/solution.py
+++ b/solution.py
@@ -30,10 +30,11 @@
 
 
 def exchange_kernel(nz, nx, nc, send, send_hot, hot_rows, hot_at, w_gate, w_up, w_down,
-                    got, got_hot, hot_terms,
+                    got, got_hot, hot_terms, cold_hidden, cold_gate, cold_up,
                     mid, mid_hot, turned, pair_gu, pair_d, one_gu, one_d, row_gu, row_d,
                     two_gu, two_d, col_gu, col_d, three_gu, three_d, full_gu, full_d,
                     hot_in, part, parts, own_terms,
+                    gate_here, up_here, down_here, slot_rows, sums,
                     z_send, z_recv, q_send, q_recv, local_sem,
                     y_send, y_recv, f_send, f_recv,
                     c_send, c_recv, x_send, x_recv, w_send, w_recv, g_send, g_recv,
@@ -284,6 +285,47 @@
         block = hot_terms.at[:, :, c]
         return remote(block, block, b_send.at[0], b_recv.at[0], twin)
 
+    here = ((w_gate, gate_here), (w_up, up_here), (w_down, down_here))
+
+    def here_copy(i):
+        return pltpu.make_async_copy(here[i][0], here[i][1], own_sem.at[12 + i])
+
+    def cold(s):
+        for k in range(nq):
+            y_copy(s, k, 1 if k < nq // 2 else 0).wait_recv()
+            f_copy(s, k).wait_recv()
+        tiles = ny * nq
+        taken = pltpu.make_async_copy(
+            got.at[:, s * tiles : (s + 1) * tiles], slot_rows, own_sem.at[15])
+        taken.start()
+        taken.wait()
+        step = slot_rows.shape[-1]
+        count = tiles * nz
+
+        def piece(n):
+            block = slot_rows[n].astype(jnp.float32)
+            return block.reshape(count, step).astype(jnp.bfloat16)
+
+        for n in range(pieces // 2):
+            cut = slice(n * step, (n + 1) * step)
+            row_tokens, row_grads = piece(n), piece(pieces // 2 + n)
+            new = (
+                jnp.dot(row_tokens, gate_here[cut, :], preferred_element_type=jnp.float32),
+                jnp.dot(row_tokens, up_here[cut, :], preferred_element_type=jnp.float32),
+                lax.dot_general(row_grads, down_here[:, cut], (((1,), (1,)), ((), ())),
+                                preferred_element_type=jnp.float32),
+            )
+            for m in range(3):
+                if n == 0:
+                    sums[m] = new[m]
+                else:
+                    sums[m] += new[m]
+        hidden, gate_grad, up_grad = terms_of(sums[0], sums[1], sums[2])
+        at = slice(s * count, (s + 1) * count)
+        cold_hidden[at, :] = hidden
+        cold_gate[at, :] = gate_grad
+        cold_up[at, :] = up_grad
+
     hot_z = hot_at[0]
     hot_x = hot_at[1]
     hot_c = hot_at[2]
@@ -302,6 +344,8 @@
         c_own(i).wait()
         c_copy(i).wait_recv()
 
+    for i in range(3):
+        here_copy(i).start()
     tile = half // 14
 
     def keep_half(n, carry):
@@ -399,9 +443,14 @@
         u_copy(k).start()
     for k in range(nq):
         pass_on(chunks, k)
+    for i in range(3):
+        here_copy(i).wait()
+    cold(0)
+    cold(1)
     for k in range(1, nx):
         u_copy(k).wait_recv()
     b_copy().start()
+    cold(2)
     b_copy().wait()
 
     for i in range(3):
@@ -428,8 +477,10 @@
         for k in range(nq):
             y_copy(s, k, 0).wait_send()
             y_copy(s, k, 1).wait_send()
-            y_copy(s, k, 1 if k < nq // 2 else 0).wait_recv()
-            f_copy(s, k).wait()
+            f_copy(s, k).wait_send()
+            if s == chunks:
+                y_copy(s, k, 1 if k < nq // 2 else 0).wait_recv()
+                f_copy(s, k).wait_recv()
 
 
 def exchange(send, send_hot, hot_rows, hot_at, w_gate, w_up, w_down, nz, nx, nc):
@@ -454,9 +505,12 @@
             jax.ShapeDtypeStruct((pieces, slots * 4 * nq, nz, wide), bf16),
             jax.ShapeDtypeStruct((nz, nq, 4, hot_slots, hot_width), bf16),
             jax.ShapeDtypeStruct((nz, nx, nc, 4 * hot_slots, 3 * width), bf16),
+            jax.ShapeDtypeStruct((slots * 4 * nq * nz, width), bf16),
+            jax.ShapeDtypeStruct((slots * 4 * nq * nz, width), bf16),
+            jax.ShapeDtypeStruct((slots * 4 * nq * nz, width), bf16),
         ),
         in_specs=[hbm, hbm, vmem, smem, hbm, hbm, hbm],
-        out_specs=(hbm, hbm, hbm),
+        out_specs=(hbm, hbm, hbm, vmem, vmem, vmem),
         scratch_shapes=[
             pltpu.VMEM((slots, nz, nq, pieces, wide), bf16),
             pltpu.VMEM((nz, nq, hot_slots, hot_width), bf16),
@@ -479,6 +533,11 @@
             pltpu.VMEM((4, nq, hot_slots, 3 * width), f32),
             pltpu.VMEM((nq, 4, hot_slots, 3 * width), f32),
             pltpu.VMEM((4 * hot_slots, 3 * width), bf16),
+            pltpu.VMEM((rows, width), bf16),
+            pltpu.VMEM((rows, width), bf16),
+            pltpu.VMEM((width, rows), bf16),
+            pltpu.VMEM((pieces, 4 * nq, nz, wide), bf16),
+            pltpu.VMEM((3, 4 * nq * nz, width), f32),
             dma((steps, nz - 1)),
             dma((steps, nz - 1)),
             dma((steps, nq - 1)),
@@ -508,10 +567,10 @@
             dma((nx - 1,)),
             dma((1,)),
             dma((1,)),
-            dma((12,)),
+            dma((16,)),
         ],
         compiler_params=pltpu.CompilerParams(
-            collective_id=0, has_side_effects=True, vmem_limit_bytes=40 * 1024 * 1024
+            collective_id=0, has_side_effects=True, vmem_limit_bytes=48 * 1024 * 1024
         ),
         cost_estimate=pl.CostEstimate(flops=0, bytes_accessed=300_000_000, transcendentals=0),
     )(send, send_hot, hot_rows, hot_at, w_gate, w_up, w_down)
@@ -577,7 +636,7 @@
         ]
     )
     hot_at = jnp.stack([hot_expert // nq, hot_expert % nq // nc, hot_expert % nc])
-    got, got_hot, hot_terms = exchange(
+    got, got_hot, hot_terms, hidden, gate_grad, up_grad = exchange(
         send.reshape(capacity, nz, nq, PIECES, width),
         send_hot.reshape(nz, nq, hot_slots, hot_width),
         hot_rows,
@@ -592,24 +651,6 @@
     rows = got.reshape(PIECES, capacity * 4 * experts, width)
     cold_tokens, cold_grads = rows[: PIECES // 2], rows[PIECES // 2 :]
     f32 = jnp.float32
-    pre_gate = sum(
-        jnp.dot(cold_tokens[n], w_gate[0, n * width : (n + 1) * width], preferred_element_type=f32)
-        for n in range(PIECES // 2)
-    )
-    pre_up = sum(
-        jnp.dot(cold_tokens[n], w_up[0, n * width : (n + 1) * width], preferred_element_type=f32)
-        for n in range(PIECES // 2)
-    )
-    hidden_back = sum(
-        lax.dot_general(
-            cold_grads[n],
-            w_down[0, :, n * width : (n + 1) * width],
-            (((1,), (1,)), ((), ())),
-            preferred_element_type=f32,
-        )
-        for n in range(PIECES // 2)
-    )
-    hidden, gate_grad, up_grad = terms_of(pre_gate, pre_up, hidden_back)
     grad_gate = lax.dot_general(
         cold_tokens, gate_grad, (((1,), (0,)), ((), ())), preferred_element_type=f32
     ).astype(jnp.bfloat16).reshape(feature_width, -1)

time: 198 us -> 196 us (0.990)
  matrix products: 21.9 us -> 18 us
  Pallas kernels: 161 us -> 163 us
    dot_general x12 -> x0, matrix products: 11.6 us -> none  [the longest x4 6.9 us: on_device(): jnp.dot(cold_tokens[n], w_gate[0, n * width:(n + 1) * width], preferred_e...]
    dot_general x5, matrix products: 3.02 us -> 9.82 us  [column_sum(): lax.dot_general(left, right, CONTRACT_ROWS, preferred_element_type=jnp.fl...]
where the time goes in v4:
time: 196 us
  Pallas kernels  163 us (83%)
  matrix products  18 us (9%)
  other arithmetic  7.73 us (4%)
  local copies, waits for them, and re-layouts  3.84 us (2%)
  between operations  3.51 us (2%)
    pallas_call x1, Pallas kernels, exchange(): pl.pallas_call(body, out_shape=(jax.ShapeDtypeStruct((pieces, slots * 4 *...  163 us
    dot_general x5, matrix products, column_sum(): lax.dot_general(left, right, CONTRACT_ROWS, preferred_element_type=jnp.fl...  9.82 us

profile of v4, /device:TPU:1, one launch (start us, length us, event | category | flops | bytes accessed | tf_op | source)
XLA Modules:
  0.0 196.0 jit_solution(8094057714384068247)
XLA Ops:
  3.3 0.1 pad_add_fusion.refs_3_
  3.4 0.1 pad.36.clone
  3.4 1.3 convert_bitcast_fusion
  4.7 0.1 copy.16
  4.9 0.2 reduce-window.8
  5.0 0.1 add_reduce_fusion
  5.1 0.8 fusion.41
  5.9 0.2 reduce_window_sum.18
  6.1 0.8 select_reduce_fusion
  6.9 0.0 copy-start.2
  6.9 0.7 multiply_add_fusion
  7.7 1.4 multiply_convert_fusion
  9.1 1.5 convolution_convert_fusion.1
  10.6 0.2 reshape.121
  10.9 0.2 reshape.122
  11.1 0.1 maximum_bitcast_fusion.1
  11.2 0.1 copy.17
  11.4 0.9 convolution_convert_fusion
  12.3 0.0 copy-start
  12.3 0.0 copy-start.1
  12.3 2.0 %copy.22 = bf16[24,8,8,896]{3,2,1,0:T(8,128)(2,1)} copy(bf16[24,8,8,896]{3,1,2,0:T(8,128)(2,1)S(1)} %bitcast.105) | data formatting | bytes 5505024
  14.4 1.0 copy-done.1
  15.4 162.9 %shard_map.111 = (bf16[8,96,8,896]{3,2,1,0:T(8,128)(2,1)}, bf16[8,8,4,8,128]{4,3,2,1,0:T(8,128)(2,1)S(1)}, bf16[8,4,2,32,768]{4,3,2,1,0:T(8,128)(2,1)}, bf16[768...) custom-call(bf16[3,8,8,8,896]{4,3,2,1,0:T(8,128)(2,1)} %bitcast.106, ...), custom_call_target="tpu_custom_call" | custom-call | bytes 300000000 | tf_op jit(solution)/shard_map/pallas_call | solution.py:502
  178.3 2.7 %convolution_convert_fusion.2 = bf16[128,768]{1,0:T(8,128)(2,1)S(1)} fusion(bf16[2048,128]{1,0:T(8,128)(2,1)S(1)} %bitcast.104, bf16[2048,768]{1,0:T(8,128)(2,1)} %bitcast.107), kind=kOutput, calls=%fused_computation.29 | convolution fusion | flops 402751488 | bytes 3866624 | tf_op jit(solution)/shard_map/dot_general | solution.py:25
  181.0 0.6 pad_maximum_fusion.3
  181.6 2.7 %fusion.33 = bf16[256,896]{1,0:T(8,128)(2,1)S(1)} fusion(bf16[768,256]{1,0:T(8,128)(2,1)S(1)} %get-tuple-element.13, bf16[8,96,8,896]{3,2,1,0:T(8,128)(2,1)} %get-tuple-element.10), kind=kOutput, calls=%fused_computation.28 | convolution fusion | flops 352550912 | bytes 2228224 | tf_op jit(solution)/shard_map/dot_general | solution.py:25
  184.3 1.9 fusion.30
  186.3 1.9 fusion.27
  188.2 0.6 fusion.24
  188.8 1.4 maximum_bitcast_fusion
  190.2 2.9 %fusion.9 = bf16[4,896,256]{2,1,0:T(8,128)(2,1)} fusion(bf16[8,96,8,896]{3,2,1,0:T(8,128)(2,1)S(1)} %copy-done.3, bf16[768,256]{1,0:T(8,128)(2,1)S(1)} %get-tuple-element.12), kind=kOutput, calls=%fused_computation.12 | convolution fusion | flops 1410203648 | bytes 7733248 | tf_op jit(solution)/shard_map/dot_general | solution.py:657
  193.1 2.9 %fusion.6 = bf16[4,896,256]{2,1,0:T(8,128)(2,1)} fusion(bf16[8,96,8,896]{3,2,1,0:T(8,128)(2,1)S(1)} %copy-done.3, bf16[768,256]{1,0:T(8,128)(2,1)S(1)} %get-tuple-element.11), kind=kOutput, calls=%fused_computation.11 | convolution fusion | flops 1410203648 | bytes 7733248 | tf_op jit(solution)/shard_map/dot_general | solution.py:654
  (19 shorter events, 0.1 us)
Async XLA Ops:
  6.9 4.5 %copy-start.2 = (bf16[128,3584]{1,0:T(8,128)(2,1)S(1)}, bf16[128,3584]{1,0:T(8,128)(2,1)}, u32[]{:S(2)}) copy-start(bf16[128,3584]{1,0:T(8,128)(2,1)} %param.8) | copy-start | bytes 2752516
  12.3 2.1 %copy-start = (bf16[1,3584,256]{2,1,0:T(8,128)(2,1)S(1)}, bf16[1,3584,256]{2,1,0:T(8,128)(2,1)}, u32[]{:S(2)}) copy-start(bf16[1,3584,256]{2,1,0:T(8,128)(2,1)} %param.13) | copy-start | bytes 5505028
  12.3 3.0 %copy-start.1 = (bf16[1,3584,256]{2,1,0:T(8,128)(2,1)S(1)}, bf16[1,3584,256]{2,1,0:T(8,128)(2,1)}, u32[]{:S(2)}) copy-start(bf16[1,3584,256]{2,1,0:T(8,128)(2,1)} %param.14) | copy-start | bytes 5505028
  178.3 9.9 %copy-start.3 = (bf16[8,96,8,896]{3,2,1,0:T(8,128)(2,1)S(1)}, bf16[8,96,8,896]{3,2,1,0:T(8,128)(2,1)}, u32[]{:S(2)}) copy-start(bf16[8,96,8,896]{3,2,1,0:T(8,128)(2,1)} %get-tuple-element.10) | copy-start | bytes 33030148

commit v5 on v4

--- a/solution.py
+++ b/solution.py
@@ -570,7 +570,7 @@
             dma((16,)),
         ],
         compiler_params=pltpu.CompilerParams(
-            collective_id=0, has_side_effects=True, vmem_limit_bytes=48 * 1024 * 1024
+            collective_id=0, has_side_effects=True, vmem_limit_bytes=36 * 1024 * 1024
         ),
         cost_estimate=pl.CostEstimate(flops=0, bytes_accessed=300_000_000, transcendentals=0),
     )(send, send_hot, hot_rows, hot_at, w_gate, w_up, w_down)

time: 196 us -> 193 us (0.985)
  matrix products: 18 us -> 15.8 us
    dot_general x5, matrix products: 9.82 us -> 7.6 us  [column_sum(): lax.dot_general(left, right, CONTRACT_ROWS, preferred_element_type=jnp.fl...]
where the time goes in v5:
time: 193 us
  Pallas kernels  163 us (84%)
  matrix products  15.8 us (8%)
  other arithmetic  7.73 us (4%)
  between operations  3.53 us (2%)
  local copies, waits for them, and re-layouts  3.39 us (2%)
    pallas_call x1, Pallas kernels, exchange(): pl.pallas_call(body, out_shape=(jax.ShapeDtypeStruct((pieces, slots * 4 *...  163 us
    dot_general x5, matrix products, column_sum(): lax.dot_general(left, right, CONTRACT_ROWS, preferred_element_type=jnp.fl...  7.6 us

profile of v5, /device:TPU:1, one launch (start us, length us, event | category | flops | bytes accessed | tf_op | source)
XLA Modules:
  0.0 192.9 jit_solution(7274378321796170261)
XLA Ops:
  3.3 0.1 pad_add_fusion.refs_3_
  3.4 0.1 pad.36.clone
  3.4 1.3 convert_bitcast_fusion
  4.7 0.1 copy.16
  4.9 0.2 reduce-window.8
  5.0 0.1 add_reduce_fusion
  5.1 0.8 fusion.41
  5.9 0.2 reduce_window_sum.18
  6.1 0.8 select_reduce_fusion
  6.9 0.0 copy-start.3
  6.9 0.7 multiply_add_fusion
  7.7 1.4 multiply_convert_fusion
  9.1 1.5 convolution_convert_fusion.1
  10.6 0.2 reshape.121
  10.9 0.2 reshape.122
  11.1 0.1 maximum_bitcast_fusion.1
  11.2 0.1 copy.17
  11.4 0.9 convolution_convert_fusion
  12.4 0.5 copy.22
  12.9 0.9 copy-done
  13.8 0.6 copy-done.1
  14.4 0.6 copy-done.2
  14.9 162.5 %shard_map.111 = (bf16[8,96,8,896]{3,2,1,0:T(8,128)(2,1)}, bf16[8,8,4,8,128]{4,3,2,1,0:T(8,128)(2,1)S(1)}, bf16[8,4,2,32,768]{4,3,2,1,0:T(8,128)(2,1)S(1)}, bf16...) custom-call(bf16[3,8,8,8,896]{4,3,2,1,0:T(8,128)(2,1)S(1)} %bitcast.101, ...), custom_call_target="tpu_custom_call" | custom-call | bytes 300000000 | tf_op jit(solution)/shard_map/pallas_call | solution.py:502
  177.5 0.6 convolution_convert_fusion.2
  178.1 0.6 pad_maximum_fusion.3
  178.8 2.5 %fusion.33 = bf16[256,896]{1,0:T(8,128)(2,1)S(1)} fusion(bf16[768,256]{1,0:T(8,128)(2,1)S(1)} %get-tuple-element.13, bf16[8,96,8,896]{3,2,1,0:T(8,128)(2,1)} %get-tuple-element.10), kind=kOutput, calls=%fused_computation.28 | convolution fusion | flops 352550912 | bytes 2228224 | tf_op jit(solution)/shard_map/dot_general | solution.py:25
  181.3 1.9 %fusion.30 = bf16[256,896]{1,0:T(8,128)(2,1)S(1)} fusion(bf16[768,256]{1,0:T(8,128)(2,1)S(1)} %get-tuple-element.13, bf16[8,96,8,896]{3,2,1,0:T(8,128)(2,1)} %get-tuple-element.10), kind=kOutput, calls=%fused_computation.27 | convolution fusion | flops 352550912 | bytes 2228224 | tf_op jit(solution)/shard_map/dot_general | solution.py:25
  183.2 1.9 %fusion.27 = bf16[256,896]{1,0:T(8,128)(2,1)S(1)} fusion(bf16[768,256]{1,0:T(8,128)(2,1)S(1)} %get-tuple-element.13, bf16[8,96,8,896]{3,2,1,0:T(8,128)(2,1)} %get-tuple-element.10), kind=kOutput, calls=%fused_computation.26 | convolution fusion | flops 352550912 | bytes 2228224 | tf_op jit(solution)/shard_map/dot_general | solution.py:25
  185.2 0.6 fusion.24
  185.8 1.4 maximum_bitcast_fusion
  187.1 2.9 %fusion.9 = bf16[4,896,256]{2,1,0:T(8,128)(2,1)} fusion(bf16[8,96,8,896]{3,2,1,0:T(8,128)(2,1)S(1)} %copy-done.4, bf16[768,256]{1,0:T(8,128)(2,1)S(1)} %get-tuple-element.12), kind=kOutput, calls=%fused_computation.12 | convolution fusion | flops 1410203648 | bytes 7733248 | tf_op jit(solution)/shard_map/dot_general | solution.py:657
  190.0 2.9 %fusion.6 = bf16[4,896,256]{2,1,0:T(8,128)(2,1)} fusion(bf16[8,96,8,896]{3,2,1,0:T(8,128)(2,1)S(1)} %copy-done.4, bf16[768,256]{1,0:T(8,128)(2,1)S(1)} %get-tuple-element.11), kind=kOutput, calls=%fused_computation.11 | convolution fusion | flops 1410203648 | bytes 7733248 | tf_op jit(solution)/shard_map/dot_general | solution.py:654
  (21 shorter events, 0.1 us)
Async XLA Ops:
  6.9 4.5 %copy-start.3 = (bf16[128,3584]{1,0:T(8,128)(2,1)S(1)}, bf16[128,3584]{1,0:T(8,128)(2,1)}, u32[]{:S(2)}) copy-start(bf16[128,3584]{1,0:T(8,128)(2,1)} %param.8) | copy-start | bytes 2752516
  12.3 1.5 copy-start
  12.3 2.0 %copy-start.1 = (bf16[1,3584,256]{2,1,0:T(8,128)(2,1)S(1)}, bf16[1,3584,256]{2,1,0:T(8,128)(2,1)}, u32[]{:S(2)}) copy-start(bf16[1,3584,256]{2,1,0:T(8,128)(2,1)} %param.14) | copy-start | bytes 5505028
  12.3 2.6 %copy-start.2 = (bf16[1,256,3584]{2,1,0:T(8,128)(2,1)S(1)}, bf16[1,256,3584]{2,1,0:T(8,128)(2,1)}, u32[]{:S(2)}) copy-start(bf16[1,256,3584]{2,1,0:T(8,128)(2,1)} %param.15) | copy-start | bytes 5505028
  177.5 7.7 %copy-start.4 = (bf16[8,96,8,896]{3,2,1,0:T(8,128)(2,1)S(1)}, bf16[8,96,8,896]{3,2,1,0:T(8,128)(2,1)}, u32[]{:S(2)}) copy-start(bf16[8,96,8,896]{3,2,1,0:T(8,128)(2,1)} %get-tuple-element.10) | copy-start | bytes 33030148
